TPU v7x, 512 devices: a whole 4x4x16 slice. The times are simulated.
512 devices in a mesh: sec: 4 (over x_lo, core), tile: 128 (over x_hi, y, z).
Axes of the slice: x: 4 (x_hi: 2, x_lo: 2; x = x_hi * 2 + x_lo), y: 4, z: 16, core: 2. Of those that a mesh axis runs over, the one named last changes fastest.
Arguments:
- ocean_u: float32 [64, 262144], P(None, ('sec', 'tile')), may hold values from -2 to 2
- ocean_b: float32 [64, 262144], P(None, ('sec', 'tile')), may hold values from -4 to 4
- tracers: bfloat16 [17, 64, 196608], P(None, None, ('sec', 'tile')), may hold values from 0.099609375 to 2
- wet_tiles: int32 [1536], replicated, may hold values from 0 to 2047, as said below
- kinetic_matrix: float32 [17, 17], replicated, may hold values from -0.42 to 1.5
Outputs:
- tracers_out: bfloat16 [17, 64, 196608], P(None, None, ('sec', 'tile'))
- ocean_u_out: float32 [64, 262144], P(None, ('sec', 'tile'))
- ocean_b_out: float32 [64, 262144], P(None, ('sec', 'tile'))
Inputs may be any that keep to these rules, and one draw needn't show every extreme that they name: `wet_tiles`: increasing tile numbers. For every k, of the tiles k * 4 to k * 4 + 3 either 2 or 4 are listed, and for every even k the tiles of k and k + 1 hold 6 listed tiles together.
All inputs are finite; a program needn't handle non-finite values.
Results may differ from a plain program's by a relative error of at most 0.001.
Values sent between devices are 32-bit elements; how exact they have to be, the bound alone decides.
A program may use at most 64 MiB of HBM per device.

v0:
```python
import jax
import jax.numpy as jnp
from jax import lax
from jax.sharding import PartitionSpec as P

TILE_COLS = 128
STEPS = 2
WET_DEV = 3
OCEAN_DEV = 4


DT_OCEAN = 0.25
PRESSURE = 1.0
HORIZ_VISC = 0.2
VERT_VISC = 0.2
HEATING = 0.2
KAPPA_BASE = 0.05
KAPPA_SPAN = 0.35
DT_TRACER = 0.3
DT_MIX = 1.0
KINETIC_DELTA = 0.5
SURFACE_LIGHT = 10.0
WATER_ATT = 0.04
PIGMENT_ATT = 0.08
GROWTH = 0.05
THERMAL_GAIN = 0.1


def partner(value, axis, stride):
    mask = 2**stride
    pairs = [(source, source ^ mask) for source in range(lax.axis_size(axis))]
    return lax.ppermute(value, axis, pairs)


def with_halo(x, sides, width):
    for axis, dim in sides:
        size, length = (lax.axis_size(axis), x.shape[dim])
        up = [(i, (i + 1) % size) for i in range(size)]
        down = [(j, i) for i, j in up]
        last = lax.slice_in_dim(x, length - width, length, axis=dim)
        leading = lax.slice_in_dim(x, 0, width, axis=dim)
        before = lax.ppermute(last, axis, up)
        after = lax.ppermute(leading, axis, down)
        x = jnp.concatenate([before, x, after], axis=dim)
    return x


def vertical_term(field):
    upper_cells = jnp.concatenate([field[:1], field[:-1]], axis=0)
    lower_cells = jnp.concatenate([field[1:], field[-1:]], axis=0)
    return upper_cells + lower_cells - 2.0 * field


def ocean_core(vel_ext, buoy_ext):
    velocity = vel_ext[:, 1:-1]
    buoyancy = buoy_ext[:, 1:-1]
    horiz_term = vel_ext[:, :-2] + vel_ext[:, 2:] - 2.0 * velocity
    press_term = buoy_ext[:, 2:] - buoyancy
    updated = velocity + DT_OCEAN * (
        HORIZ_VISC * horiz_term + VERT_VISC * vertical_term(velocity) - PRESSURE * press_term
    )
    return (updated, buoyancy)


def diffusivity_of(velocity, buoyancy):
    shear_sq = (velocity[:-1] - velocity[1:]) ** 2
    stratified = buoyancy[:-1] - buoyancy[1:]
    interior = KAPPA_BASE + KAPPA_SPAN * jax.nn.sigmoid(4.0 * (shear_sq - stratified))
    return jnp.concatenate([interior, jnp.zeros_like(interior[:1])], axis=0)


def absorption_of(tracer_state):
    pigment = tracer_state[0]
    attenuation = WATER_ATT + PIGMENT_ATT * pigment * pigment
    optical_depth = jnp.cumsum(attenuation, axis=0)
    return SURFACE_LIGHT * (jnp.exp(attenuation - optical_depth) - jnp.exp(-optical_depth))


def profile_change(
    transported_solutes, turbulent_spreading, seawater_warmth, captured_radiance, kinetic_matrix
):
    lower_cells = jnp.concatenate([transported_solutes[:, 1:], transported_solutes[:, -1:]], axis=1)
    vert_flux = turbulent_spreading[None] * (lower_cells - transported_solutes)
    upper_flux = jnp.concatenate([jnp.zeros_like(vert_flux[:, :1]), vert_flux[:, :-1]], axis=1)
    depth_blended_fields = transported_solutes + DT_MIX * (vert_flux - upper_flux)
    kinetic_drift = jnp.einsum(
        "ij,jlc->ilc", kinetic_matrix, depth_blended_fields, precision=lax.Precision.HIGHEST
    )
    converted_solutes = (
        depth_blended_fields
        + KINETIC_DELTA * jnp.exp(THERMAL_GAIN * seawater_warmth)[None] * kinetic_drift
    )
    return jnp.concatenate(
        [converted_solutes[:1] + GROWTH * captured_radiance[None], converted_solutes[1:]], axis=0
    )


def on_device(ocean_u, ocean_b, tracers, wet_tiles, kinetic_matrix):
    levels = ocean_u.shape[0]
    device_count = lax.axis_size("sec") * lax.axis_size("tile")
    total_tiles = OCEAN_DEV * device_count
    total_wet = WET_DEV * device_count
    device = lax.axis_index("sec") * lax.axis_size("tile") + lax.axis_index("tile")
    slot_ids = device * WET_DEV + jnp.arange(WET_DEV, dtype=jnp.int32)
    slot_tiles = wet_tiles[slot_ids]
    slot_local = slot_tiles // OCEAN_DEV == device
    slot_block = jnp.where(slot_local, slot_tiles % OCEAN_DEV, OCEAN_DEV)
    own_tiles = device * OCEAN_DEV + jnp.arange(OCEAN_DEV, dtype=jnp.int32)
    own_wet = jnp.any(wet_tiles[None, :] == own_tiles[:, None], axis=1)
    own_pos = jnp.sum((wet_tiles[None, :] < own_tiles[:, None]).astype(jnp.int32), axis=1)
    own_extra = jnp.logical_and(own_wet, own_pos // WET_DEV != device)
    own_kept = jnp.logical_and(own_wet, jnp.logical_not(own_extra))
    own_slot = jnp.clip(own_pos - device * WET_DEV, 0, WET_DEV - 1)
    beside_all = jnp.mod(device * WET_DEV - 1 + jnp.arange(WET_DEV + 2, dtype=jnp.int32), total_wet)
    around_tiles = wet_tiles[beside_all]
    adjacent = (jnp.mod(around_tiles[1:] - around_tiles[:-1], total_tiles) == 1).astype(jnp.float32)
    face_open = jnp.ones((WET_DEV + 1, TILE_COLS), jnp.float32).at[:, 0].set(adjacent)
    face_open = face_open.reshape((WET_DEV + 1) * TILE_COLS)[: WET_DEV * TILE_COLS + 1]
    tracer_state = tracers.astype(jnp.float32)
    velocity = ocean_u
    buoyancy = ocean_b
    for step_index in range(STEPS):
        captured_radiance = absorption_of(tracer_state)
        slot_light = captured_radiance.reshape(levels, WET_DEV, TILE_COLS)
        send_back = jnp.sum(
            jnp.where(jnp.logical_not(slot_local)[None, :, None], slot_light, 0.0), axis=1
        )
        returned = partner(send_back, "tile", 0)
        kept_light = jnp.take(slot_light, own_slot, axis=1)
        heating_term = jnp.where(
            own_kept[None, :, None],
            kept_light,
            jnp.where(own_extra[None, :, None], returned[:, None, :], 0.0),
        )
        buoyancy = buoyancy + HEATING * heating_term.reshape(levels, OCEAN_DEV * TILE_COLS)
        ocean_ext = with_halo(jnp.stack([velocity, buoyancy]), ((("sec", "tile"), 2),), 1)
        velocity, buoyancy = ocean_core(ocean_ext[0], ocean_ext[1])
        turbulent_spreading = diffusivity_of(velocity, buoyancy)
        fields = jnp.stack([velocity, turbulent_spreading, buoyancy]).reshape(
            3, levels, OCEAN_DEV, TILE_COLS
        )
        payload = jnp.sum(jnp.where(own_extra[None, None, :, None], fields, 0.0), axis=2)
        arrived = partner(payload, "tile", 0)
        choose = jnp.concatenate([fields, arrived[:, :, None, :]], axis=2)
        coupled = jnp.take(choose, slot_block, axis=2).reshape(3, levels, WET_DEV * TILE_COLS)
        halo_in = jnp.concatenate([tracer_state, coupled[:1]], axis=0)
        extended = with_halo(halo_in, ((("sec", "tile"), 2),), 1)
        ext_state = extended[:-1]
        face_u = extended[-1][:, :-1]
        face_flux = (
            jnp.maximum(face_u, 0.0) * ext_state[:, :, :-1]
            + jnp.minimum(face_u, 0.0) * ext_state[:, :, 1:]
        ) * face_open
        transported_solutes = tracer_state - DT_TRACER * (
            face_flux[:, :, 1:] - face_flux[:, :, :-1]
        )
        tracer_state = profile_change(
            transported_solutes, coupled[1], coupled[2], captured_radiance, kinetic_matrix
        )
    return (tracer_state.astype(jnp.bfloat16), velocity, buoyancy)


def solution(mesh):
    placed = (
        P(None, ("sec", "tile")),
        P(None, ("sec", "tile")),
        P(None, None, ("sec", "tile")),
        P(),
        P(),
    )
    return jax.shard_map(
        on_device,
        mesh=mesh,
        in_specs=placed,
        out_specs=(
            P(None, None, ("sec", "tile")),
            P(None, ("sec", "tile")),
            P(None, ("sec", "tile")),
        ),
        check_vma=False,
    )
```

profile of v0, /device:TPU:1, one launch (start us, length us, event | category | flops | bytes accessed | tf_op | source)
XLA Modules:
  0.0 118.6 jit_solution(4158292073337790829)
XLA Ops:
  1.5 1.3 %convert_element_type.10 = f32[17,64,384]{2,1,0:T(8,128)S(1)} convert(bf16[17,64,384]{2,1,0:T(8,128)(2,1)} %param.13) | non-fusion elementwise | flops 417792 | bytes 2506752 | tf_op jit(solution)/shard_map/convert_element_type | solution.py:119
  3.9 4.4 %collective-permute-start = (f32[64,128]{1,0:T(8,128)S(1)}, f32[64,128]{1,0:T(8,128)S(1)}, u32[]{:S(2)}, u32[]{:S(2)}) collective-permute-start(f32[64,128]{1,0:T(8,128)S(1)} %get-tuple-element.45), channel_id=1, source_target_pairs={{0,1},{1,0},{2,3},{3,2},{4,5},{5,4},{6,7},{7,6},{8,9},{9,8},{10,11... | collective-permute-start | bytes 98312 | tf_op jit(solution)/shard_map/ppermute | solution.py:32
  10.8 2.3 %collective-permute-start.1 = (f32[2,64,1]{2,1,0:T(8,128)S(1)}, f32[2,64,1]{2,1,0:T(8,128)S(1)}, u32[]{:S(2)}, u32[]{:S(2)}) collective-permute-start(f32[2,64,1]{2,1,0:T(8,128)S(1)} %get-tuple-element.63), channel_id=1, source_target_pairs={{0,1},{1,2},{2,3},{3,4},{4,5},{5,6},{6,7},{7,8},{8,9},{9,10},{10,1... | collective-permute-start | bytes 1544 | tf_op jit(solution)/shard_map/ppermute | solution.py:42
  13.1 16.1 %collective-permute-start.2 = (f32[2,64,1]{2,1,0:T(8,128)S(1)}, f32[2,64,1]{2,1,0:T(8,128)S(1)}, u32[]{:S(2)}, u32[]{:S(2)}) collective-permute-start(f32[2,64,1]{2,1,0:T(8,128)S(1)} %get-tuple-element.64), channel_id=1, source_target_pairs={{1,0},{2,1},{3,2},{4,3},{5,4},{6,5},{7,6},{8,7},{9,8},{10,9},{11,1... | collective-permute-start | bytes 1544 | tf_op jit(solution)/shard_map/ppermute | solution.py:43
  31.9 1.9 %collective-permute-start.3 = (f32[3,64,128]{2,1,0:T(8,128)S(1)}, f32[3,64,128]{2,1,0:T(8,128)S(1)}, u32[]{:S(2)}, u32[]{:S(2)}) collective-permute-start(f32[3,64,128]{2,1,0:T(8,128)S(1)} %select_reduce_fusion.1), channel_id=1, source_target_pairs={{0,1},{1,0},{2,3},{3,2},{4,5},{5,4},{6,7},{7,6},{8,9},{9,8},{10,11... | collective-permute-start | bytes 294920 | tf_op jit(solution)/shard_map/ppermute | solution.py:32
  33.8 4.3 %collective-permute-done.3 = f32[3,64,128]{2,1,0:T(8,128)S(1)} collective-permute-done((f32[3,64,128]{2,1,0:T(8,128)S(1)}, f32[3,64,128]{2,1,0:T(8,128)S(1)}, u32[]{:S(2)}, u32[]{:S(2)}) %collective-permute-start.3) | collective-permute-done | bytes 98336 | tf_op jit(solution)/shard_map/ppermute | solution.py:32
  39.6 10.2 %collective-permute-start.5 = (f32[18,64,1]{1,2,0:T(1,128)S(1)}, f32[18,64,1]{1,2,0:T(1,128)S(1)}, u32[]{:S(2)}, u32[]{:S(2)}) collective-permute-start(f32[18,64,1]{1,2,0:T(1,128)S(1)} %copy.161), channel_id=1, source_target_pairs={{1,0},{2,1},{3,2},{4,3},{5,4},{6,5},{7,6},{8,7},{9,8},{10,9},{11,1... | collective-permute-start | bytes 13832 | tf_op jit(solution)/shard_map/ppermute | solution.py:43
  49.9 1.9 %collective-permute-start.4 = (f32[18,64,1]{1,2,0:T(1,128)S(1)}, f32[18,64,1]{1,2,0:T(1,128)S(1)}, u32[]{:S(2)}, u32[]{:S(2)}) collective-permute-start(f32[18,64,1]{1,2,0:T(1,128)S(1)} %copy.160), channel_id=1, source_target_pairs={{0,1},{1,2},{2,3},{3,4},{4,5},{5,6},{6,7},{7,8},{8,9},{9,10},{10,1... | collective-permute-start | bytes 13832 | tf_op jit(solution)/shard_map/ppermute | solution.py:42
  52.6 7.9 %collective-permute-done.4 = f32[18,64,1]{1,2,0:T(1,128)S(1)} collective-permute-done((f32[18,64,1]{1,2,0:T(1,128)S(1)}, f32[18,64,1]{1,2,0:T(1,128)S(1)}, u32[]{:S(2)}, u32[]{:S(2)}) %collective-permute-start.4) | collective-permute-done | bytes 4640 | tf_op jit(solution)/shard_map/ppermute | solution.py:42
  63.9 3.1 %fusion.2 = f32[64,384,17]{1,2,0:T(8,128)S(1)} fusion(f32[17,64,384]{2,1,0:T(8,128)S(1)} %subtract_add_fusion.1, f32[17,17]{1,0:T(8,128)S(1)} %copy-done), kind=kOutput, calls=%fused_computation.8 | convolution fusion | flops 85229568 | bytes 3343492 | tf_op jit(solution)/shard_map/ij,jlc->ilc/dot_general | solution.py:86
  68.2 1.0 reduce_window_sum.28
  70.0 1.9 %collective-permute-start.6 = (f32[64,128]{1,0:T(8,128)S(1)}, f32[64,128]{1,0:T(8,128)S(1)}, u32[]{:S(2)}, u32[]{:S(2)}) collective-permute-start(f32[64,128]{1,0:T(8,128)S(1)} %get-tuple-element.34), channel_id=1, source_target_pairs={{0,1},{1,0},{2,3},{3,2},{4,5},{5,4},{6,7},{7,6},{8,9},{9,8},{10,11... | collective-permute-start | bytes 98312 | tf_op jit(solution)/shard_map/ppermute | solution.py:32
  72.6 2.0 %collective-permute-done.6 = f32[64,128]{1,0:T(8,128)S(1)} collective-permute-done((f32[64,128]{1,0:T(8,128)S(1)}, f32[64,128]{1,0:T(8,128)S(1)}, u32[]{:S(2)}, u32[]{:S(2)}) %collective-permute-start.6) | collective-permute-done | bytes 32800 | tf_op jit(solution)/shard_map/ppermute | solution.py:32
  74.7 1.0 fusion.18
  75.7 0.9 pad_maximum_fusion.28
  76.6 1.9 %collective-permute-start.7 = (f32[2,64,1]{2,1,0:T(8,128)S(1)}, f32[2,64,1]{2,1,0:T(8,128)S(1)}, u32[]{:S(2)}, u32[]{:S(2)}) collective-permute-start(f32[2,64,1]{2,1,0:T(8,128)S(1)} %get-tuple-element.61), channel_id=1, source_target_pairs={{0,1},{1,2},{2,3},{3,4},{4,5},{5,6},{6,7},{7,8},{8,9},{9,10},{10,1... | collective-permute-start | bytes 1544 | tf_op jit(solution)/shard_map/ppermute | solution.py:42
  78.5 9.4 %collective-permute-start.8 = (f32[2,64,1]{2,1,0:T(8,128)S(1)}, f32[2,64,1]{2,1,0:T(8,128)S(1)}, u32[]{:S(2)}, u32[]{:S(2)}) collective-permute-start(f32[2,64,1]{2,1,0:T(8,128)S(1)} %get-tuple-element.62), channel_id=1, source_target_pairs={{1,0},{2,1},{3,2},{4,3},{5,4},{6,5},{7,6},{8,7},{9,8},{10,9},{11,1... | collective-permute-start | bytes 1544 | tf_op jit(solution)/shard_map/ppermute | solution.py:43
  87.9 1.3 %collective-permute-done.8 = f32[2,64,1]{2,1,0:T(8,128)S(1)} collective-permute-done((f32[2,64,1]{2,1,0:T(8,128)S(1)}, f32[2,64,1]{2,1,0:T(8,128)S(1)}, u32[]{:S(2)}, u32[]{:S(2)}) %collective-permute-start.8) | collective-permute-done | bytes 544 | tf_op jit(solution)/shard_map/ppermute | solution.py:43
  90.5 1.9 %collective-permute-start.9 = (f32[3,64,128]{2,1,0:T(8,128)S(1)}, f32[3,64,128]{2,1,0:T(8,128)S(1)}, u32[]{:S(2)}, u32[]{:S(2)}) collective-permute-start(f32[3,64,128]{2,1,0:T(8,128)S(1)} %select_reduce_fusion), channel_id=1, source_target_pairs={{0,1},{1,0},{2,3},{3,2},{4,5},{5,4},{6,7},{7,6},{8,9},{9,8},{10,11... | collective-permute-start | bytes 294920 | tf_op jit(solution)/shard_map/ppermute | solution.py:32
  92.6 3.3 %collective-permute-done.9 = f32[3,64,128]{2,1,0:T(8,128)S(1)} collective-permute-done((f32[3,64,128]{2,1,0:T(8,128)S(1)}, f32[3,64,128]{2,1,0:T(8,128)S(1)}, u32[]{:S(2)}, u32[]{:S(2)}) %collective-permute-start.9) | collective-permute-done | bytes 98336 | tf_op jit(solution)/shard_map/ppermute | solution.py:32
  97.2 1.9 %collective-permute-start.10 = (f32[18,64,1]{1,2,0:T(1,128)S(1)}, f32[18,64,1]{1,2,0:T(1,128)S(1)}, u32[]{:S(2)}, u32[]{:S(2)}) collective-permute-start(f32[18,64,1]{1,2,0:T(1,128)S(1)} %copy.180), channel_id=1, source_target_pairs={{0,1},{1,2},{2,3},{3,4},{4,5},{5,6},{6,7},{7,8},{8,9},{9,10},{10,1... | collective-permute-start | bytes 13832 | tf_op jit(solution)/shard_map/ppermute | solution.py:42
  99.4 11.3 %collective-permute-start.11 = (f32[18,64,1]{1,2,0:T(1,128)S(1)}, f32[18,64,1]{1,2,0:T(1,128)S(1)}, u32[]{:S(2)}, u32[]{:S(2)}) collective-permute-start(f32[18,64,1]{1,2,0:T(1,128)S(1)} %copy.181), channel_id=1, source_target_pairs={{1,0},{2,1},{3,2},{4,3},{5,4},{6,5},{7,6},{8,7},{9,8},{10,9},{11,1... | collective-permute-start | bytes 13832 | tf_op jit(solution)/shard_map/ppermute | solution.py:43
  113.9 3.1 %fusion = f32[64,384,17]{1,2,0:T(8,128)S(1)} fusion(f32[17,64,384]{2,1,0:T(8,128)S(1)} %subtract_add_fusion, f32[17,17]{1,0:T(8,128)S(1)} %copy-done), kind=kOutput, calls=%fused_computation.6 | convolution fusion | flops 85229568 | bytes 3343492 | tf_op jit(solution)/shard_map/ij,jlc->ilc/dot_general | solution.py:86
  117.6 1.0 pad_maximum_fusion.10
  (153 shorter events, 21.3 us)
Async XLA Ops:
  0.6 63.3 %copy-start = (f32[17,17]{1,0:T(8,128)S(1)}, f32[17,17]{1,0:T(8,128)}, u32[]{:S(2)}) copy-start(f32[17,17]{1,0:T(8,128)} %param.15) | copy-start | bytes 3472
  2.8 7.8 %copy-start.10 = (f32[64,512]{1,0:T(8,128)S(1)}, f32[64,512]{1,0:T(8,128)}, u32[]{:S(2)}) copy-start(f32[64,512]{1,0:T(8,128)} %param.12) | copy-start | bytes 393220
  2.8 7.8 %copy-start.8 = (f32[64,512]{1,0:T(8,128)S(1)}, f32[64,512]{1,0:T(8,128)}, u32[]{:S(2)}) copy-start(f32[64,512]{1,0:T(8,128)} %param.11) | copy-start | bytes 393220
  3.5 35.2 %copy-start.17 = (pred[3]{0:T(512)(128)(4,1)}, pred[3]{0:T(512)(128)(4,1)S(1)}, u32[]{:S(2)}) copy-start(pred[3]{0:T(512)(128)(4,1)S(1)} %get-tuple-element.38) | copy-start | bytes 13
  3.6 5.1 %copy-start.19 = (pred[3]{0:T(512)(128)(4,1)}, pred[3]{0:T(512)(128)(4,1)S(1)}, u32[]{:S(2)}) copy-start(pred[3]{0:T(512)(128)(4,1)S(1)} %compare_not_fusion) | copy-start | bytes 13
  3.9 6.7 %collective-permute-start = (f32[64,128]{1,0:T(8,128)S(1)}, f32[64,128]{1,0:T(8,128)S(1)}, u32[]{:S(2)}, u32[]{:S(2)}) collective-permute-start(f32[64,128]{1,0:T(8,128)S(1)} %get-tuple-element.45), channel_id=1, source_target_pairs={{0,1},{1,0},{2,3},{3,2},{4,5},{5,4},{6,7},{7,6},{8,9},{9,8},{10,11... | collective-permute-start | bytes 98312 | tf_op jit(solution)/shard_map/ppermute | solution.py:32
  8.7 22.3 %copy-start.15 = (pred[4]{0:T(512)(128)(4,1)}, pred[4]{0:T(512)(128)(4,1)S(1)}, u32[]{:S(2)}) copy-start(pred[4]{0:T(512)(128)(4,1)S(1)} %get-tuple-element.41) | copy-start | bytes 16
  8.7 22.3 %copy-start.16 = (pred[4]{0:T(512)(128)(4,1)}, pred[4]{0:T(512)(128)(4,1)S(1)}, u32[]{:S(2)}) copy-start(pred[4]{0:T(512)(128)(4,1)S(1)} %get-tuple-element.79) | copy-start | bytes 16
  8.7 23.1 %copy-start.11 = (pred[4]{0:T(512)(128)(4,1)}, pred[4]{0:T(512)(128)(4,1)S(1)}, u32[]{:S(2)}) copy-start(pred[4]{0:T(512)(128)(4,1)S(1)} %get-tuple-element.42) | copy-start | bytes 16
  8.7 22.3 %copy-start.13 = (s32[1024]{0:T(1024)}, s32[1024]{0:T(1024)S(1)}, u32[]{:S(2)}) copy-start(s32[1024]{0:T(1024)S(1)} %pad_clamp_fusion.2) | copy-start | bytes 12292
  10.8 19.3 %collective-permute-start.1 = (f32[2,64,1]{2,1,0:T(8,128)S(1)}, f32[2,64,1]{2,1,0:T(8,128)S(1)}, u32[]{:S(2)}, u32[]{:S(2)}) collective-permute-start(f32[2,64,1]{2,1,0:T(8,128)S(1)} %get-tuple-element.63), channel_id=1, source_target_pairs={{0,1},{1,2},{2,3},{3,4},{4,5},{5,6},{6,7},{7,8},{8,9},{9,10},{10,1... | collective-permute-start | bytes 1544 | tf_op jit(solution)/shard_map/ppermute | solution.py:42
  13.1 17.4 %collective-permute-start.2 = (f32[2,64,1]{2,1,0:T(8,128)S(1)}, f32[2,64,1]{2,1,0:T(8,128)S(1)}, u32[]{:S(2)}, u32[]{:S(2)}) collective-permute-start(f32[2,64,1]{2,1,0:T(8,128)S(1)} %get-tuple-element.64), channel_id=1, source_target_pairs={{1,0},{2,1},{3,2},{4,3},{5,4},{6,5},{7,6},{8,7},{9,8},{10,9},{11,1... | collective-permute-start | bytes 1544 | tf_op jit(solution)/shard_map/ppermute | solution.py:43
  31.2 7.0 %copy-start.2 = (f32[64,512]{1,0:T(8,128)}, f32[64,512]{1,0:T(8,128)S(1)}, u32[]{:S(2)}) copy-start(f32[64,512]{1,0:T(8,128)S(1)} %get-tuple-element.70) | copy-start | bytes 393220
  31.9 6.3 %collective-permute-start.3 = (f32[3,64,128]{2,1,0:T(8,128)S(1)}, f32[3,64,128]{2,1,0:T(8,128)S(1)}, u32[]{:S(2)}, u32[]{:S(2)}) collective-permute-start(f32[3,64,128]{2,1,0:T(8,128)S(1)} %select_reduce_fusion.1), channel_id=1, source_target_pairs={{0,1},{1,0},{2,3},{3,2},{4,5},{5,4},{6,7},{7,6},{8,9},{9,8},{10,11... | collective-permute-start | bytes 294920 | tf_op jit(solution)/shard_map/ppermute | solution.py:32
  33.8 5.3 %copy-start.14 = (s32[1024]{0:T(1024)}, s32[1024]{0:T(1024)S(1)}, u32[]{:S(2)}) copy-start(s32[1024]{0:T(1024)S(1)} %pad_clamp_fusion.1) | copy-start | bytes 12292
  39.6 21.2 %collective-permute-start.5 = (f32[18,64,1]{1,2,0:T(1,128)S(1)}, f32[18,64,1]{1,2,0:T(1,128)S(1)}, u32[]{:S(2)}, u32[]{:S(2)}) collective-permute-start(f32[18,64,1]{1,2,0:T(1,128)S(1)} %copy.161), channel_id=1, source_target_pairs={{1,0},{2,1},{3,2},{4,3},{5,4},{6,5},{7,6},{8,7},{9,8},{10,9},{11,1... | collective-permute-start | bytes 13832 | tf_op jit(solution)/shard_map/ppermute | solution.py:43
  49.9 10.7 %collective-permute-start.4 = (f32[18,64,1]{1,2,0:T(1,128)S(1)}, f32[18,64,1]{1,2,0:T(1,128)S(1)}, u32[]{:S(2)}, u32[]{:S(2)}) collective-permute-start(f32[18,64,1]{1,2,0:T(1,128)S(1)} %copy.160), channel_id=1, source_target_pairs={{0,1},{1,2},{2,3},{3,4},{4,5},{5,6},{6,7},{7,8},{8,9},{9,10},{10,1... | collective-permute-start | bytes 13832 | tf_op jit(solution)/shard_map/ppermute | solution.py:42
  68.2 21.0 %copy-start.3 = (f32[64,512]{1,0:T(8,128)S(1)}, f32[64,512]{1,0:T(8,128)}, u32[]{:S(2)}) copy-start(f32[64,512]{1,0:T(8,128)} %copy-done.2) | copy-start | bytes 393220
  70.0 4.7 %collective-permute-start.6 = (f32[64,128]{1,0:T(8,128)S(1)}, f32[64,128]{1,0:T(8,128)S(1)}, u32[]{:S(2)}, u32[]{:S(2)}) collective-permute-start(f32[64,128]{1,0:T(8,128)S(1)} %get-tuple-element.34), channel_id=1, source_target_pairs={{0,1},{1,0},{2,3},{3,2},{4,5},{5,4},{6,7},{7,6},{8,9},{9,8},{10,11... | collective-permute-start | bytes 98312 | tf_op jit(solution)/shard_map/ppermute | solution.py:32
  76.6 11.3 %collective-permute-start.7 = (f32[2,64,1]{2,1,0:T(8,128)S(1)}, f32[2,64,1]{2,1,0:T(8,128)S(1)}, u32[]{:S(2)}, u32[]{:S(2)}) collective-permute-start(f32[2,64,1]{2,1,0:T(8,128)S(1)} %get-tuple-element.61), channel_id=1, source_target_pairs={{0,1},{1,2},{2,3},{3,4},{4,5},{5,6},{6,7},{7,8},{8,9},{9,10},{10,1... | collective-permute-start | bytes 1544 | tf_op jit(solution)/shard_map/ppermute | solution.py:42
  78.5 10.7 %collective-permute-start.8 = (f32[2,64,1]{2,1,0:T(8,128)S(1)}, f32[2,64,1]{2,1,0:T(8,128)S(1)}, u32[]{:S(2)}, u32[]{:S(2)}) collective-permute-start(f32[2,64,1]{2,1,0:T(8,128)S(1)} %get-tuple-element.62), channel_id=1, source_target_pairs={{1,0},{2,1},{3,2},{4,3},{5,4},{6,5},{7,6},{8,7},{9,8},{10,9},{11,1... | collective-permute-start | bytes 1544 | tf_op jit(solution)/shard_map/ppermute | solution.py:43
  90.5 5.3 %collective-permute-start.9 = (f32[3,64,128]{2,1,0:T(8,128)S(1)}, f32[3,64,128]{2,1,0:T(8,128)S(1)}, u32[]{:S(2)}, u32[]{:S(2)}) collective-permute-start(f32[3,64,128]{2,1,0:T(8,128)S(1)} %select_reduce_fusion), channel_id=1, source_target_pairs={{0,1},{1,0},{2,3},{3,2},{4,5},{5,4},{6,7},{7,6},{8,9},{9,8},{10,11... | collective-permute-start | bytes 294920 | tf_op jit(solution)/shard_map/ppermute | solution.py:32
  97.2 13.7 %collective-permute-start.10 = (f32[18,64,1]{1,2,0:T(1,128)S(1)}, f32[18,64,1]{1,2,0:T(1,128)S(1)}, u32[]{:S(2)}, u32[]{:S(2)}) collective-permute-start(f32[18,64,1]{1,2,0:T(1,128)S(1)} %copy.180), channel_id=1, source_target_pairs={{0,1},{1,2},{2,3},{3,4},{4,5},{5,6},{6,7},{7,8},{8,9},{9,10},{10,1... | collective-permute-start | bytes 13832 | tf_op jit(solution)/shard_map/ppermute | solution.py:42
  99.4 11.9 %collective-permute-start.11 = (f32[18,64,1]{1,2,0:T(1,128)S(1)}, f32[18,64,1]{1,2,0:T(1,128)S(1)}, u32[]{:S(2)}, u32[]{:S(2)}) collective-permute-start(f32[18,64,1]{1,2,0:T(1,128)S(1)} %copy.181), channel_id=1, source_target_pairs={{1,0},{2,1},{3,2},{4,3},{5,4},{6,5},{7,6},{8,7},{9,8},{10,9},{11,1... | collective-permute-start | bytes 13832 | tf_op jit(solution)/shard_map/ppermute | solution.py:43
  (8 other events, 13.3 us)
where the time goes:
time: 120 us; the launch traced here: 119 us
  starting transfers between devices  65.2 us (54%)
  waiting for transfers between devices  19.5 us (16%)
  other arithmetic  16 us (13%)
  local copies, waits for them, and re-layouts  9.98 us (8%)
  matrix products  6.26 us (5%)
  between operations  1.64 us (1%)
    ppermute x4, starting transfers between devices, with_halo(): after = lax.ppermute(leading, axis, down)  47 us
    ppermute x4, starting transfers between devices, partner(): return lax.ppermute(value, axis, pairs)  10.1 us
    ppermute x4, waiting for transfers between devices, partner(): return lax.ppermute(value, axis, pairs)  9.64 us
    ppermute x4, starting transfers between devices, with_halo(): before = lax.ppermute(last, axis, up)  8.06 us
    ppermute x4, waiting for transfers between devices, with_halo(): before = lax.ppermute(last, axis, up)  7.96 us
    dot_general x2, matrix products, profile_change(): jnp.einsum('ij,jlc->ilc', kinetic_matrix, depth_blended_fields, precision...  6.26 us
  transfers between devices with their start and end apart: 12, of which 7 were waited for; matrix products, arithmetic and copies ran while one was open for 5% of the time, Pallas kernels for 0%

commit v1 on v0

v1 whole, which is shorter than its diff:
```python
import functools

import jax
import jax.numpy as jnp
from jax import lax
from jax.experimental import pallas as pl
from jax.experimental.pallas import tpu as pltpu
from jax.sharding import PartitionSpec as P

MESH = pl.DeviceIdType.MESH
LANES = 128
STEPS = 2
WET_DEV = 3
OCEAN_DEV = 4
HALO = 3

DT_OCEAN = 0.25
PRESSURE = 1.0
HORIZ_VISC = 0.2
VERT_VISC = 0.2
HEATING = 0.2
KAPPA_BASE = 0.05
KAPPA_SPAN = 0.35
DT_TRACER = 0.3
DT_MIX = 1.0
KINETIC_DELTA = 0.5
SURFACE_LIGHT = 10.0
WATER_ATT = 0.04
PIGMENT_ATT = 0.08
GROWTH = 0.05
THERMAL_GAIN = 0.1


def roll(x, shift, axis):
    size = x.shape[axis]
    shift = shift % size
    return x if shift == 0 else pltpu.roll(x, shift, axis)


def iota(shape, axis):
    return lax.broadcasted_iota(jnp.int32, shape, axis)


def pick(position, options):
    value = None
    for where, option in options:
        value = option if value is None else jnp.where(position == where, option, value)
    return value


def kernel(
    secs, tiles, u_in, b_in, t_in, wet_in, k_in,
    t_out, u_out, b_out,
    u_v, b_v, t_v, k_v, wet_s, to_left, to_right, from_left, from_right, far_in, far_back,
    s_v, mix_v, abs_v, coef, out_v, ub_out, load_sem, wet_sem, send_sem, recv_sem, store_sem,
):
    levels = u_in.shape[0]
    tracers = t_in.shape[0]
    padded = mix_v.shape[0]
    total_wet = WET_DEV * secs * tiles
    total_tiles = OCEAN_DEV * secs * tiles
    own = OCEAN_DEV * LANES
    slots = WET_DEV * LANES
    sec = lax.axis_index("sec")
    tile = lax.axis_index("tile")
    device = sec * tiles + tile
    right_flat = lax.rem(device + 1, secs * tiles)
    left_flat = lax.rem(device + secs * tiles - 1, secs * tiles)
    right = (right_flat // tiles, lax.rem(right_flat, tiles))
    left = (left_flat // tiles, lax.rem(left_flat, tiles))
    odd = lax.rem(tile, 2)
    partner = (sec, tile + 1 - 2 * odd)
    even_lane = odd == 0

    barrier = pltpu.get_barrier_semaphore()
    for neighbour in (left, right):
        pl.semaphore_signal(barrier, inc=1, device_id=neighbour, device_id_type=MESH)

    loads = [
        pltpu.make_async_copy(t_in, t_v, load_sem.at[0]),
        pltpu.make_async_copy(u_in, u_v.at[:, pl.ds(0, own)], load_sem.at[1]),
        pltpu.make_async_copy(b_in, b_v.at[:, pl.ds(0, own)], load_sem.at[2]),
        pltpu.make_async_copy(k_in, k_v, load_sem.at[3]),
        pltpu.make_async_copy(wet_in, wet_s, wet_sem),
    ]
    for load in loads:
        load.start()

    def remote(src, dst, index, target):
        return pltpu.make_async_remote_copy(
            src_ref=src, dst_ref=dst, send_sem=send_sem.at[index], recv_sem=recv_sem.at[index],
            device_id=target, device_id_type=MESH,
        )

    edge = pl.ds(pl.multiple_of((own - LANES) * (1 - odd), LANES), LANES)
    far_u = remote(u_in.at[:, edge], far_in.at[0], 2, partner)
    far_b = remote(b_in.at[:, edge], far_in.at[1], 3, partner)

    lane = iota((levels, LANES), 1)
    loads[0].wait()
    first = jnp.zeros((levels, LANES), jnp.float32)
    last = jnp.zeros((levels, LANES), jnp.float32)
    for t in range(tracers):
        here = (lane >= 2 * t) & (lane < 2 * t + 2)
        head = t_v[t, :, :LANES].astype(jnp.float32)
        tail = t_v[t, :, slots - LANES :].astype(jnp.float32)
        first = jnp.where(here, roll(head, 2 * t, 1), first)
        last = jnp.where(here, roll(tail, 2 * t + 2, 1), last)
    loads[1].wait()
    loads[2].wait()
    base = 2 * tracers
    for field, offset in ((u_v, base), (b_v, base + HALO)):
        here = (lane >= offset) & (lane < offset + HALO)
        head = jnp.where(even_lane, field[:, :LANES], field[:, LANES : 2 * LANES])
        tail = jnp.where(even_lane, field[:, 2 * LANES : 3 * LANES], field[:, 3 * LANES : own])
        first = jnp.where(here, roll(head, offset, 1), first)
        last = jnp.where(here, roll(tail, offset + HALO, 1), last)
    to_left[...] = first
    to_right[...] = last

    pl.semaphore_wait(barrier, 2)
    near_left = remote(to_left, from_right, 0, left)
    near_right = remote(to_right, from_left, 1, right)
    near_left.start()
    near_right.start()
    far_u.start()
    far_b.start()

    loads[3].wait()
    rows = 8 * padded
    spread = ((iota((rows, tracers), 0) >> 3) == iota((rows, tracers), 1)).astype(jnp.float32)
    wide = 3 * rows
    column = iota((tracers, wide), 1)
    column = jnp.where(column >= 2 * rows, column - 2 * rows, jnp.where(column >= rows, column - rows, column))
    gather = ((column >> 3) == iota((tracers, wide), 0)).astype(jnp.float32)
    exact = functools.partial(
        jnp.dot, precision=lax.Precision.HIGHEST, preferred_element_type=jnp.float32
    )
    matrix = exact(exact(spread, k_v[...]), gather)
    same = (iota((rows, wide), 0) & 7) == (iota((rows, wide), 1) & 7)
    matrix = jnp.where(same, matrix, 0.0)
    coarse = matrix.astype(jnp.bfloat16)
    fine = (matrix - coarse.astype(jnp.float32)).astype(jnp.bfloat16)
    matrix = jnp.where(iota((rows, wide), 1) < 2 * rows, coarse.astype(jnp.float32), fine.astype(jnp.float32)).astype(jnp.bfloat16)
    mix_v[tracers, :, :] = jnp.zeros(mix_v.shape[1:], jnp.float32)

    for t in range(tracers):
        s_v[t, :, :slots] = t_v[t].astype(jnp.float32)

    loads[4].wait()
    listed = [
        wet_s[lax.rem(device * WET_DEV + total_wet + j, total_wet)] for j in range(-1, WET_DEV + 1)
    ]
    ring = OCEAN_DEV + 2
    relative = [lax.rem(w - device * OCEAN_DEV + total_tiles + 2, total_tiles) - 2 for w in listed]
    position = [
        jnp.where(r < 0, r + ring, jnp.where(r < ring, r, ring)) for r in relative
    ]
    is_open = [
        lax.rem(listed[j + 1] - listed[j] + total_tiles, total_tiles) == 1 for j in range(WET_DEV + 1)
    ]
    spot_left, spot, spot_right = position[0], position[1 : WET_DEV + 1], position[WET_DEV + 1]

    tri = (iota((levels, levels), 0) >= iota((levels, levels), 1)).astype(jnp.float32)

    def absorb(width, start):
        pigment = s_v[0, :, start : start + width]
        attenuation = WATER_ATT + PIGMENT_ATT * pigment * pigment
        depth = exact(tri, attenuation)
        below = jnp.exp(-depth)
        above = jnp.where(iota((levels, width), 0) == 0, 1.0, roll(below, 1, 0))
        abs_v[:, start : start + width] = SURFACE_LIGHT * (above - below)

    absorb(slots, 0)

    near_left.wait()
    near_right.wait()
    for t in range(tracers):
        after = roll(from_right[...], -2 * t, 1)
        before = roll(from_left[...], -2 - 2 * t, 1)
        s_v[t, :, slots:] = jnp.where(lane < 2, after, jnp.where(lane >= LANES - 2, before, 0.0))
    absorb(LANES, slots)
    far_u.wait()
    far_b.wait()
    for field, offset, far in ((u_v, base, far_in[0]), (b_v, base + HALO, far_in[1])):
        after = roll(from_right[...], -offset, 1)
        before = roll(from_left[...], -HALO - offset, 1)
        near = jnp.where(lane < HALO, after, jnp.where(lane >= LANES - HALO, before, 0.0))
        field[:, own : own + LANES] = jnp.where(even_lane, far, near)
        field[:, own + LANES :] = jnp.where(even_lane, near, far)

    final = None
    for step in range(STEPS):
        width = slots + LANES if step < STEPS - 1 else slots
        light = [abs_v[:, j * LANES : (j + 1) * LANES] for j in range(WET_DEV + 1)]
        heat = []
        for q in range(ring):
            at_halo = jnp.where(lane < LANES // 2, spot_right, spot_left) == q
            term = jnp.where(at_halo, light[WET_DEV], 0.0)
            for j in range(WET_DEV):
                term = jnp.where(spot[j] == q, light[j], term)
            heat.append(term)
        buoyancy = b_v[...] + HEATING * jnp.concatenate(heat, axis=1)
        b_v[...] = buoyancy
        velocity = u_v[...]
        level = iota(velocity.shape, 0)
        horiz = roll(velocity, 1, 1) + roll(velocity, -1, 1) - 2.0 * velocity
        press = roll(buoyancy, -1, 1) - buoyancy
        upper = jnp.where(level == 0, velocity, roll(velocity, 1, 0))
        lower = jnp.where(level == levels - 1, velocity, roll(velocity, -1, 0))
        vert = upper + lower - 2.0 * velocity
        u_v[...] = velocity + DT_OCEAN * (
            HORIZ_VISC * horiz + VERT_VISC * vert - PRESSURE * press
        )
        if step == STEPS - 1:
            place = pl.ds(pl.multiple_of(own + LANES * odd, LANES), LANES)
            final = (
                remote(u_v.at[:, place], far_back.at[0], 4, partner),
                remote(b_v.at[:, place], far_back.at[1], 5, partner),
            )
            for copy in final:
                copy.start()
        taken = []
        for field in (u_v, b_v):
            part = [field[:, q * LANES : (q + 1) * LANES] for q in range(ring)]
            chosen = [
                pick(spot[0], [(0, part[0]), (1, part[1]), (2, part[2]), (5, part[5])]),
                pick(spot[1], [(0, part[0]), (1, part[1]), (2, part[2]), (3, part[3])]),
                pick(spot[2], [(1, part[1]), (2, part[2]), (3, part[3]), (4, part[4])]),
            ]
            ahead = pick(spot_right, [(3, part[3]), (4, part[4]), (5, part[5])])
            behind = pick(spot_left, [(0, part[0]), (4, part[4]), (5, part[5])])
            chosen.append(jnp.where(lane < LANES // 2, ahead, behind))
            taken.append(jnp.concatenate(chosen, axis=1))
        face_u, warmth = taken
        level = iota(face_u.shape, 0)
        shear = face_u - roll(face_u, -1, 0)
        stratified = warmth - roll(warmth, -1, 0)
        steep = 4.0 * (shear * shear - stratified)
        spreading = KAPPA_BASE + KAPPA_SPAN / (1.0 + jnp.exp(-steep))
        spreading = jnp.where(level == levels - 1, 0.0, spreading)
        spreading_up = jnp.where(level == 0, 0.0, roll(spreading, 1, 0))
        gates = []
        for j in range(WET_DEV + 1):
            ends = is_open[(j + 1) % (WET_DEV + 1)].astype(jnp.float32)
            gates.append(jnp.where(lane == LANES - 1, ends, 1.0))
        gate = DT_TRACER * jnp.concatenate(gates, axis=1)
        forward = jnp.maximum(face_u, 0.0) * gate
        backward = jnp.minimum(face_u, 0.0) * gate
        forward_in = roll(forward, 1, 1)
        coef[0] = 1.0 - forward + roll(backward, 1, 1)
        coef[1] = -backward
        coef[2] = forward_in
        coef[3] = 1.0 - DT_MIX * (spreading + spreading_up)
        coef[4] = DT_MIX * spreading
        coef[5] = DT_MIX * spreading_up
        coef[6] = KINETIC_DELTA * jnp.exp(THERMAL_GAIN * warmth)

        for t in range(tracers):
            state = s_v[t]
            moved = (
                coef[0] * state + coef[1] * roll(state, -1, 1) + coef[2] * roll(state, 1, 1)
            )[:, :width]
            mixed = (
                coef[3][:, :width] * moved
                + coef[4][:, :width] * roll(moved, -1, 0)
                + coef[5][:, :width] * roll(moved, 1, 0)
            )
            mix_v[t, :, :width] = mixed

        for group in range(levels // 16):
            halves = []
            for half in range(2):
                level = slice(group * 16 + half * 8, group * 16 + half * 8 + 8)
                mixed = mix_v[:, level, :width]
                flat = mixed.reshape(rows, width)
                high = flat.astype(jnp.bfloat16)
                low = (flat - high.astype(jnp.float32)).astype(jnp.bfloat16)
                drift = jnp.dot(
                    matrix, jnp.concatenate([high, low, high], axis=0),
                    preferred_element_type=jnp.float32,
                ).reshape(padded, 8, width)
                grown = mixed + coef[6, level, :width][None] * drift
                grown_first = grown[0] + GROWTH * abs_v[level, :width]
                grown = jnp.concatenate([grown_first[None], grown[1:tracers]], axis=0)
                if step < STEPS - 1:
                    s_v[:, level, :width] = grown
                halves.append(grown)
            if step == STEPS - 1:
                level = slice(group * 16, group * 16 + 16)
                out_v[:, level, :] = jnp.concatenate(halves, axis=1).astype(jnp.bfloat16)
        if step < STEPS - 1:
            absorb(width, 0)

    store_t = pltpu.make_async_copy(out_v, t_out, store_sem.at[0])
    store_t.start()
    for copy in final:
        copy.wait()
    for field, index in ((u_v, 0), (b_v, 1)):
        back = far_back[index]
        low_given = jnp.logical_and(odd == 1, spot_left == 0)
        high_given = jnp.logical_and(odd == 0, spot_right == OCEAN_DEV - 1)
        ub_out[index, :, :LANES] = jnp.where(low_given, back, field[:, :LANES])
        ub_out[index, :, LANES : own - LANES] = field[:, LANES : own - LANES]
        ub_out[index, :, own - LANES :] = jnp.where(high_given, back, field[:, own - LANES : own])
    store_u = pltpu.make_async_copy(ub_out.at[0], u_out, store_sem.at[1])
    store_b = pltpu.make_async_copy(ub_out.at[1], b_out, store_sem.at[2])
    store_u.start()
    store_b.start()
    store_t.wait()
    store_u.wait()
    store_b.wait()


def on_device(ocean_u, ocean_b, tracers, wet_tiles, kinetic_matrix):
    levels, own = ocean_u.shape
    count, _, slots = tracers.shape
    padded = count + count % 2
    wide = slots + LANES
    domain = own + 2 * LANES
    f32 = jnp.float32
    anywhere = pl.BlockSpec(memory_space=pl.ANY)
    return pl.pallas_call(
        functools.partial(kernel, lax.axis_size("sec"), lax.axis_size("tile")),
        out_shape=(
            jax.ShapeDtypeStruct(tracers.shape, jnp.bfloat16),
            jax.ShapeDtypeStruct(ocean_u.shape, f32),
            jax.ShapeDtypeStruct(ocean_b.shape, f32),
        ),
        in_specs=[anywhere] * 5,
        out_specs=(anywhere,) * 3,
        scratch_shapes=[
            pltpu.VMEM((levels, domain), f32),
            pltpu.VMEM((levels, domain), f32),
            pltpu.VMEM(tracers.shape, jnp.bfloat16),
            pltpu.VMEM(kinetic_matrix.shape, f32),
            pltpu.SMEM(wet_tiles.shape, jnp.int32),
            pltpu.VMEM((levels, LANES), f32),
            pltpu.VMEM((levels, LANES), f32),
            pltpu.VMEM((levels, LANES), f32),
            pltpu.VMEM((levels, LANES), f32),
            pltpu.VMEM((2, levels, LANES), f32),
            pltpu.VMEM((2, levels, LANES), f32),
            pltpu.VMEM((count, levels, wide), f32),
            pltpu.VMEM((padded, levels, wide), f32),
            pltpu.VMEM((levels, wide), f32),
            pltpu.VMEM((7, levels, wide), f32),
            pltpu.VMEM(tracers.shape, jnp.bfloat16),
            pltpu.VMEM((2, levels, own), f32),
            pltpu.SemaphoreType.DMA((4,)),
            pltpu.SemaphoreType.DMA,
            pltpu.SemaphoreType.DMA((6,)),
            pltpu.SemaphoreType.DMA((6,)),
            pltpu.SemaphoreType.DMA((3,)),
        ],
        compiler_params=pltpu.CompilerParams(
            collective_id=0, has_side_effects=True, vmem_limit_bytes=48 * 2**20
        ),
    )(ocean_u, ocean_b, tracers, wet_tiles, kinetic_matrix)


def solution(mesh):
    flat = ("sec", "tile")
    placed = (P(None, flat), P(None, flat), P(None, None, flat), P(), P())
    return jax.shard_map(
        on_device,
        mesh=mesh,
        in_specs=placed,
        out_specs=(P(None, None, flat), P(None, flat), P(None, flat)),
        check_vma=False,
    )
```

time: 120 us -> 33.9 us (0.28)
  starting transfers between devices: 65.2 us -> 0 us
  Pallas kernels: 0 us -> 26.4 us
  waiting for transfers between devices: 19.5 us -> 0 us
  other arithmetic: 16 us -> 0 us
  matrix products: 6.26 us -> 0 us
  local copies, waits for them, and re-layouts: 9.98 us -> 6.56 us
    ppermute x12 -> x0, starting transfers between devices: 65.2 us -> none  [the longest x4 47 us: with_halo(): after = lax.ppermute(leading, axis, down)]
    pallas_call x0 -> x1, Pallas kernels: none -> 26.4 us  [on_device(): pl.pallas_call(functools.partial(kernel, lax.axis_size('sec'), lax.axis_s...]
    ppermute x12 -> x0, waiting for transfers between devices: 19.5 us -> none  [the longest x4 9.64 us: partner(): return lax.ppermute(value, axis, pairs)]
    dot_general x2 -> x0, matrix products: 6.26 us -> none  [profile_change(): jnp.einsum('ij,jlc->ilc', kinetic_matrix, depth_blended_fields, precision...]
    unnamed x49 -> x13, local copies, waits for them, and re-layouts: 1.69 us -> 6.56 us
    gather x6 -> x0, local copies, waits for them, and re-layouts: 3.76 us -> none  [the longest x2 1.25 us: on_device(): jnp.take(choose, slot_block, axis=2).reshape(3, levels, WET_DEV * TILE_COLS)]
    another operation x7 -> x0, other arithmetic: 3.72 us -> none
    slice x19 -> x0, local copies, waits for them, and re-layouts: 2.89 us -> none  [the longest x1 0.81 us: absorption_of(): pigment = tracer_state[0]]
  transfers between devices with their start and end apart: 12 -> 0, of which waited for: 7 -> 0; matrix products, arithmetic and copies ran while one was open for 5% -> 0% of each run, Pallas kernels for 0% -> 0%
where the time goes in v1:
time: 33.9 us; the launch traced here: 33.7 us
  Pallas kernels  26.4 us (78%)
  local copies, waits for them, and re-layouts  6.56 us (19%)
  between operations  0.65 us (2%)
    pallas_call x1, Pallas kernels, on_device(): pl.pallas_call(functools.partial(kernel, lax.axis_size('sec'), lax.axis_s...  26.4 us
    unnamed x13, local copies, waits for them, and re-layouts  6.56 us

profile of v1, /device:TPU:1, one launch (start us, length us, event | category | flops | bytes accessed | tf_op | source)
XLA Modules:
  0.0 33.7 jit_solution(4367257682216456946)
XLA Ops:
  0.6 0.0 copy-start
  0.6 1.1 %copy-done = bf16[17,64,384]{2,1,0:T(8,128)(2,1)S(1)} copy-done((bf16[17,64,384]{2,1,0:T(8,128)(2,1)S(1)}, bf16[17,64,384]{2,1,0:T(8,128)(2,1)}, u32[]{:S(2)}) %copy-start) | copy-done | bytes 835608
  1.8 0.0 copy-start.1
  1.8 0.9 %copy-done.1 = f32[64,512]{1,0:T(8,128)S(1)} copy-done((f32[64,512]{1,0:T(8,128)S(1)}, f32[64,512]{1,0:T(8,128)}, u32[]{:S(2)}) %copy-start.1) | copy-done | bytes 131096
  2.7 0.0 copy-start.2
  2.7 0.9 %copy-done.2 = f32[64,512]{1,0:T(8,128)S(1)} copy-done((f32[64,512]{1,0:T(8,128)S(1)}, f32[64,512]{1,0:T(8,128)}, u32[]{:S(2)}) %copy-start.2) | copy-done | bytes 131096
  3.6 0.0 copy-start.3
  3.6 0.7 %copy-done.3 = f32[17,17]{1,0:T(8,128)S(1)} copy-done((f32[17,17]{1,0:T(8,128)S(1)}, f32[17,17]{1,0:T(8,128)}, u32[]{:S(2)}) %copy-start.3) | copy-done | bytes 1180
  4.3 0.0 copy-start.4
  4.3 0.7 %copy-done.4 = s32[1536]{0:T(1024)S(1)} copy-done((s32[1536]{0:T(1024)S(1)}, s32[1536]{0:T(1024)}, u32[]{:S(2)}) %copy-start.4) | copy-done | bytes 6168
  5.0 26.4 %shard_map.76 = (bf16[17,64,384]{2,1,0:T(8,128)(2,1)S(1)}, f32[64,512]{1,0:T(8,128)S(1)}, f32[64,512]{1,0:T(8,128)S(1)}) custom-call(f32[64,512]{1,0:T(8,128)S(1)} %copy-done.1, f32[64,512]{1,0:T(8,128)S(1)} %copy-done.2, bf16[17,64,384]{2,1,0:T(8,128)(2,1)S(1)} %copy-done, s32[1536]{0:T(1024)S(1)} %copy-done.4, f32[17,17]{1,0:T(8,128)S(1)} %copy-done.3), custom_call_target="tpu_custom_call" | custom-call | tf_op jit(solution)/shard_map/pallas_call | solution.py:323
  31.5 0.9 %copy.11 = bf16[17,64,384]{2,1,0:T(8,128)(2,1)} copy(bf16[17,64,384]{2,1,0:T(8,128)(2,1)S(1)} %get-tuple-element.6) | data formatting | bytes 1671168
  32.3 0.7 %copy.12 = f32[64,512]{1,0:T(8,128)} copy(f32[64,512]{1,0:T(8,128)S(1)} %get-tuple-element.7) | data formatting | bytes 262144
  33.0 0.7 %copy.13 = f32[64,512]{1,0:T(8,128)} copy(f32[64,512]{1,0:T(8,128)S(1)} %get-tuple-element.8) | data formatting | bytes 262144
Async XLA Ops:
  0.6 1.2 %copy-start = (bf16[17,64,384]{2,1,0:T(8,128)(2,1)S(1)}, bf16[17,64,384]{2,1,0:T(8,128)(2,1)}, u32[]{:S(2)}) copy-start(bf16[17,64,384]{2,1,0:T(8,128)(2,1)} %t_in.1) | copy-start | bytes 2506756
  1.8 0.9 %copy-start.1 = (f32[64,512]{1,0:T(8,128)S(1)}, f32[64,512]{1,0:T(8,128)}, u32[]{:S(2)}) copy-start(f32[64,512]{1,0:T(8,128)} %u_in.1) | copy-start | bytes 393220
  2.7 0.9 %copy-start.2 = (f32[64,512]{1,0:T(8,128)S(1)}, f32[64,512]{1,0:T(8,128)}, u32[]{:S(2)}) copy-start(f32[64,512]{1,0:T(8,128)} %b_in.1) | copy-start | bytes 393220
  3.6 0.7 %copy-start.3 = (f32[17,17]{1,0:T(8,128)S(1)}, f32[17,17]{1,0:T(8,128)}, u32[]{:S(2)}) copy-start(f32[17,17]{1,0:T(8,128)} %k_in.1) | copy-start | bytes 3472
  4.3 0.7 %copy-start.4 = (s32[1536]{0:T(1024)S(1)}, s32[1536]{0:T(1024)}, u32[]{:S(2)}) copy-start(s32[1536]{0:T(1024)} %wet_in.1) | copy-start | bytes 18436

commit v2 on v1

v2 whole, which is shorter than its diff:
```python
import functools

import jax
import jax.numpy as jnp
from jax import lax
from jax.experimental import pallas as pl
from jax.experimental.pallas import tpu as pltpu
from jax.sharding import PartitionSpec as P

MESH = pl.DeviceIdType.MESH
LANES = 128
STEPS = 2
WET_DEV = 3
OCEAN_DEV = 4
HALO = 3

DT_OCEAN = 0.25
PRESSURE = 1.0
HORIZ_VISC = 0.2
VERT_VISC = 0.2
HEATING = 0.2
KAPPA_BASE = 0.05
KAPPA_SPAN = 0.35
DT_TRACER = 0.3
DT_MIX = 1.0
KINETIC_DELTA = 0.5
SURFACE_LIGHT = 10.0
WATER_ATT = 0.04
PIGMENT_ATT = 0.08
GROWTH = 0.05
THERMAL_GAIN = 0.1


def roll(x, shift, axis):
    size = x.shape[axis]
    shift = shift % size
    return x if shift == 0 else pltpu.roll(x, shift, axis)


def iota(shape, axis):
    return lax.broadcasted_iota(jnp.int32, shape, axis)


def pick(position, options):
    value = None
    for where, option in options:
        value = option if value is None else jnp.where(position == where, option, value)
    return value


def exact(a, b):
    return jnp.dot(a, b, precision=lax.Precision.HIGHEST, preferred_element_type=jnp.float32)


def absorbed_light(pigment, tri):
    attenuation = WATER_ATT + PIGMENT_ATT * pigment * pigment
    below = jnp.exp(-exact(tri, attenuation))
    above = jnp.where(iota(pigment.shape, 0) == 0, 1.0, roll(below, 1, 0))
    return SURFACE_LIGHT * (above - below)


def advance_velocity(velocity, buoyancy):
    level = iota(velocity.shape, 0)
    horiz = roll(velocity, 1, 1) + roll(velocity, -1, 1) - 2.0 * velocity
    press = roll(buoyancy, -1, 1) - buoyancy
    upper = jnp.where(level == 0, velocity, roll(velocity, 1, 0))
    lower = jnp.where(level == velocity.shape[0] - 1, velocity, roll(velocity, -1, 0))
    vert = upper + lower - 2.0 * velocity
    return velocity + DT_OCEAN * (HORIZ_VISC * horiz + VERT_VISC * vert - PRESSURE * press)


def set_coefficients(coef, face_u, warmth, gate):
    level = iota(face_u.shape, 0)
    shear = face_u - roll(face_u, -1, 0)
    stratified = warmth - roll(warmth, -1, 0)
    steep = 4.0 * (shear * shear - stratified)
    spreading = KAPPA_BASE + KAPPA_SPAN / (1.0 + jnp.exp(-steep))
    spreading = jnp.where(level == face_u.shape[0] - 1, 0.0, spreading)
    spreading_up = jnp.where(level == 0, 0.0, roll(spreading, 1, 0))
    gate = DT_TRACER * gate
    forward = jnp.maximum(face_u, 0.0) * gate
    backward = jnp.minimum(face_u, 0.0) * gate
    coef[0] = 1.0 - forward + roll(backward, 1, 1)
    coef[1] = -backward
    coef[2] = roll(forward, 1, 1)
    coef[3] = 1.0 - DT_MIX * (spreading + spreading_up)
    coef[4] = DT_MIX * spreading
    coef[5] = DT_MIX * spreading_up
    coef[6] = KINETIC_DELTA * jnp.exp(THERMAL_GAIN * warmth)


def transport(state, coef, width):
    moved = (coef[0] * state + coef[1] * roll(state, -1, 1) + coef[2] * roll(state, 1, 1))[:, :width]
    return (
        coef[3][:, :width] * moved
        + coef[4][:, :width] * roll(moved, -1, 0)
        + coef[5][:, :width] * roll(moved, 1, 0)
    )


def react(mixed, warm, light, matrix, tracers):
    padded, rows, width = mixed.shape
    flat = mixed.reshape(padded * rows, width)
    high = flat.astype(jnp.bfloat16)
    low = (flat - high.astype(jnp.float32)).astype(jnp.bfloat16)
    drift = jnp.dot(
        matrix, jnp.concatenate([high, low, high], axis=0), preferred_element_type=jnp.float32
    ).reshape(padded, rows, width)
    grown = mixed + warm[None] * drift
    return jnp.concatenate([(grown[0] + GROWTH * light)[None], grown[1:tracers]], axis=0)


def kernel(
    secs, tiles, u_in, b_in, t_in, wet_in, k_in,
    out_v, ub_out,
    u_v, b_v, t_v, k_v, wet_s, edge_t, edge_ub, to_near, to_far, from_near, from_far, tile_in, tile_back,
    s_v, mix_v, abs_v, coef, strip_v, strip_mix, strip_coef,
    load_sem, wet_sem, send_sem, recv_sem, ready_sem,
):
    levels = u_in.shape[0]
    tracers = t_in.shape[0]
    padded = mix_v.shape[0]
    total_wet = WET_DEV * secs * tiles
    total_tiles = OCEAN_DEV * secs * tiles
    own = OCEAN_DEV * LANES
    slots = WET_DEV * LANES
    sec = lax.axis_index("sec")
    tile = lax.axis_index("tile")
    device = sec * tiles + tile
    odd = lax.rem(tile, 2)
    even_lane = odd == 0
    partner = (sec, tile + 1 - 2 * odd)
    far_flat = lax.rem(device + 2 * odd - 1 + secs * tiles, secs * tiles)
    far = (far_flat // tiles, lax.rem(far_flat, tiles))

    barrier = pltpu.get_barrier_semaphore()
    pl.semaphore_signal(barrier, inc=1, device_id=partner, device_id_type=MESH)

    @pl.when(odd == 0)
    def _():
        pl.semaphore_signal(barrier, inc=1, device_id=far, device_id_type=MESH)

    slot_edge = pl.ds(pl.multiple_of((slots - LANES) * odd, LANES), LANES)
    far_edge = pl.ds(pl.multiple_of((own - LANES) * odd, LANES), LANES)
    near_edge = pl.ds(pl.multiple_of((own - LANES) * (1 - odd), LANES), LANES)
    loads = [
        pltpu.make_async_copy(t_in.at[:, :, slot_edge], edge_t, load_sem.at[0]),
        pltpu.make_async_copy(u_in.at[:, far_edge], edge_ub.at[0], load_sem.at[1]),
        pltpu.make_async_copy(b_in.at[:, far_edge], edge_ub.at[1], load_sem.at[2]),
        pltpu.make_async_copy(t_in, t_v, load_sem.at[3]),
        pltpu.make_async_copy(u_in, u_v.at[:, pl.ds(0, own)], load_sem.at[4]),
        pltpu.make_async_copy(b_in, b_v.at[:, pl.ds(0, own)], load_sem.at[5]),
        pltpu.make_async_copy(k_in, k_v, load_sem.at[6]),
        pltpu.make_async_copy(wet_in, wet_s, wet_sem),
    ]
    for load in loads:
        load.start()

    def remote(src, dst, index, target):
        return pltpu.make_async_remote_copy(
            src_ref=src, dst_ref=dst, send_sem=send_sem.at[index], recv_sem=recv_sem.at[index],
            device_id=target, device_id_type=MESH,
        )

    lane = iota((levels, LANES), 1)
    base = 2 * tracers
    for load in loads[:3]:
        load.wait()
    message = jnp.zeros((levels, LANES), jnp.float32)
    for t in range(tracers):
        here = (lane >= 2 * t) & (lane < 2 * t + 2)
        message = jnp.where(here, pltpu.roll(edge_t[t].astype(jnp.float32), 2 * t + 2 * odd, 1), message)
    for field in range(2):
        offset = base + HALO * field
        here = (lane >= offset) & (lane < offset + HALO)
        message = jnp.where(here, pltpu.roll(edge_ub[field], offset + HALO * odd, 1), message)
    to_far[...] = message

    pl.semaphore_wait(barrier, 1 + odd)
    send_far = remote(to_far, from_far, 0, far)

    @pl.when(odd == 1)
    def _():
        pl.semaphore_signal(ready_sem, inc=1, device_id=far, device_id_type=MESH)
        send_far.start()

    tile_u = remote(u_in.at[:, near_edge], tile_in.at[0], 2, partner)
    tile_b = remote(b_in.at[:, near_edge], tile_in.at[1], 3, partner)
    tile_u.start()
    tile_b.start()

    for load in loads[3:6]:
        load.wait()
    message = jnp.zeros((levels, LANES), jnp.float32)
    for t in range(tracers):
        here = (lane >= 2 * t) & (lane < 2 * t + 2)
        near = jnp.where(even_lane, t_v[t, :, slots - LANES :], t_v[t, :, :LANES]).astype(jnp.float32)
        message = jnp.where(here, pltpu.roll(near, 2 * t + 2 - 2 * odd, 1), message)
    for field, offset in ((u_v, base), (b_v, base + HALO)):
        here = (lane >= offset) & (lane < offset + HALO)
        near = jnp.where(even_lane, field[:, 2 * LANES : 3 * LANES], field[:, LANES : 2 * LANES])
        message = jnp.where(here, pltpu.roll(near, offset + HALO - HALO * odd, 1), message)
    to_near[...] = message
    send_near = remote(to_near, from_near, 1, partner)
    send_near.start()

    loads[6].wait()
    rows = 8 * padded
    wide = 3 * rows
    spread = ((iota((rows, tracers), 0) >> 3) == iota((rows, tracers), 1)).astype(jnp.float32)
    column = iota((tracers, wide), 1)
    column = jnp.where(column >= 2 * rows, column - 2 * rows, jnp.where(column >= rows, column - rows, column))
    gather = ((column >> 3) == iota((tracers, wide), 0)).astype(jnp.float32)
    matrix = exact(exact(spread, k_v[...]), gather)
    same = (iota((rows, wide), 0) & 7) == (iota((rows, wide), 1) & 7)
    matrix = jnp.where(same, matrix, 0.0)
    coarse = matrix.astype(jnp.bfloat16).astype(jnp.float32)
    matrix = jnp.where(iota((rows, wide), 1) < 2 * rows, coarse, matrix - coarse).astype(jnp.bfloat16)
    mix_v[tracers, :, :] = jnp.zeros(mix_v.shape[1:], jnp.float32)
    strip_mix[tracers, :, :] = jnp.zeros(strip_mix.shape[1:], jnp.float32)

    for t in range(tracers):
        s_v[t, :, :slots] = t_v[t].astype(jnp.float32)

    loads[7].wait()
    listed = [
        wet_s[lax.rem(device * WET_DEV + total_wet + j, total_wet)] for j in range(-1, WET_DEV + 1)
    ]
    ring = OCEAN_DEV + 2
    relative = [lax.rem(w - device * OCEAN_DEV + total_tiles + 2, total_tiles) - 2 for w in listed]
    position = [jnp.where(r < 0, r + ring, jnp.where(r < ring, r, ring)) for r in relative]
    is_open = [
        lax.rem(listed[j + 1] - listed[j] + total_tiles, total_tiles) == 1 for j in range(WET_DEV + 1)
    ]
    spot_left, spot, spot_right = position[0], position[1 : WET_DEV + 1], position[WET_DEV + 1]

    tri = (iota((levels, levels), 0) >= iota((levels, levels), 1)).astype(jnp.float32)
    abs_v[:, :slots] = absorbed_light(s_v[0, :, :slots], tri)

    send_near.wait()
    halo_two = jnp.where(even_lane, lane, LANES - 1 - lane) < 2
    halo_three = jnp.where(even_lane, lane, LANES - 1 - lane) < HALO
    for t in range(tracers):
        came = pltpu.roll(from_near[...], 2 * LANES - 2 * t - 2 * odd, 1)
        s_v[t, :, slots:] = jnp.where(halo_two, came, 0.0)
    abs_v[:, slots:] = absorbed_light(s_v[0, :, slots:], tri)
    tile_u.wait()
    tile_b.wait()
    for field, offset, whole in ((u_v, base, tile_in[0]), (b_v, base + HALO, tile_in[1])):
        came = pltpu.roll(from_near[...], 2 * LANES - offset - HALO * odd, 1)
        near = jnp.where(halo_three, came, 0.0)
        field[:, own : own + LANES] = jnp.where(even_lane, whole, near)
        field[:, own + LANES :] = jnp.where(even_lane, near, whole)

    final = None
    for step in range(STEPS):
        width = slots + LANES if step < STEPS - 1 else slots
        light = [abs_v[:, j * LANES : (j + 1) * LANES] for j in range(WET_DEV + 1)]
        heat = []
        for q in range(ring):
            at_halo = jnp.where(lane < LANES // 2, spot_right, spot_left) == q
            term = jnp.where(at_halo, light[WET_DEV], 0.0)
            for j in range(WET_DEV):
                term = jnp.where(spot[j] == q, light[j], term)
            heat.append(term)
        buoyancy = b_v[...] + HEATING * jnp.concatenate(heat, axis=1)
        b_v[...] = buoyancy
        u_v[...] = advance_velocity(u_v[...], buoyancy)
        if step == STEPS - 1:
            place = pl.ds(pl.multiple_of(own + LANES * odd, LANES), LANES)
            final = (
                remote(u_v.at[:, place], tile_back.at[0], 4, partner),
                remote(b_v.at[:, place], tile_back.at[1], 5, partner),
            )
            for copy in final:
                copy.start()
        taken = []
        for field in (u_v, b_v):
            part = [field[:, q * LANES : (q + 1) * LANES] for q in range(ring)]
            chosen = [
                pick(spot[0], [(0, part[0]), (1, part[1]), (2, part[2]), (5, part[5])]),
                pick(spot[1], [(0, part[0]), (1, part[1]), (2, part[2]), (3, part[3])]),
                pick(spot[2], [(1, part[1]), (2, part[2]), (3, part[3]), (4, part[4])]),
            ]
            ahead = pick(spot_right, [(3, part[3]), (4, part[4]), (5, part[5])])
            behind = pick(spot_left, [(0, part[0]), (4, part[4]), (5, part[5])])
            chosen.append(jnp.where(lane < LANES // 2, ahead, behind))
            taken.append(jnp.concatenate(chosen, axis=1))
        gates = []
        for j in range(WET_DEV + 1):
            ends = is_open[(j + 1) % (WET_DEV + 1)].astype(jnp.float32)
            gates.append(jnp.where(lane == LANES - 1, ends, 1.0))
        set_coefficients(coef, taken[0], taken[1], jnp.concatenate(gates, axis=1))
        for t in range(tracers):
            mix_v[t, :, :width] = transport(s_v[t], coef, width)
        for group in range(levels // 16):
            halves = []
            for half in range(2):
                level = slice(group * 16 + half * 8, group * 16 + half * 8 + 8)
                grown = react(
                    mix_v[:, level, :width], coef[6, level, :width], abs_v[level, :width], matrix, tracers
                )
                if step < STEPS - 1:
                    s_v[:, level, :width] = grown
                halves.append(grown)
            if step == STEPS - 1:
                level = slice(group * 16, group * 16 + 16)
                out_v[:, level, :] = jnp.concatenate(halves, axis=1).astype(jnp.bfloat16)
        if step < STEPS - 1:
            abs_v[:, :width] = absorbed_light(s_v[0, :, :width], tri)

    @pl.when(odd == 0)
    def _():
        pl.semaphore_wait(ready_sem, 1)
        send_far.start()

    for copy in final:
        copy.wait()
    for field, index in ((u_v, 0), (b_v, 1)):
        back = tile_back[index]
        low_given = jnp.logical_and(odd == 1, spot_left == 0)
        high_given = jnp.logical_and(odd == 0, spot_right == OCEAN_DEV - 1)
        ub_out[index, :, :LANES] = jnp.where(low_given, back, field[:, :LANES])
        ub_out[index, :, LANES : own - LANES] = field[:, LANES : own - LANES]
        ub_out[index, :, own - LANES :] = jnp.where(high_given, back, field[:, own - LANES : own])

    edge_wet = jnp.where(even_lane, relative[1] == 0, relative[WET_DEV] == OCEAN_DEV - 1)
    halo_wet = jnp.where(even_lane, relative[0] == -1, relative[WET_DEV + 1] == OCEAN_DEV)
    own_side = jnp.where(even_lane, lane, LANES - 1 - lane) < LANES // 2
    lit = jnp.where(own_side, edge_wet.astype(jnp.int32), halo_wet.astype(jnp.int32)) == 1
    ends = jnp.logical_and(edge_wet, halo_wet).astype(jnp.float32)
    gate = jnp.where(lane == LANES - 1, ends, 1.0)
    halo_two = jnp.where(even_lane, LANES - 1 - lane, lane) < 2
    halo_three = jnp.where(even_lane, LANES - 1 - lane, lane) < HALO
    result = jnp.where(even_lane, lane, LANES - 1 - lane) < 4
    send_far.wait()
    for t in range(tracers):
        came = pltpu.roll(from_far[...], 2 * LANES - 2 - 2 * t + 2 * odd, 1)
        strip_v[t] = jnp.where(halo_two, came, edge_t[t].astype(jnp.float32))
    strip = []
    for field in range(2):
        came = pltpu.roll(from_far[...], 2 * LANES - HALO - base - HALO * field + HALO * odd, 1)
        strip.append(jnp.where(halo_three, came, edge_ub[field]))
    velocity, buoyancy = strip
    for step in range(STEPS):
        light = absorbed_light(strip_v[0], tri)
        buoyancy = buoyancy + HEATING * jnp.where(lit, light, 0.0)
        velocity = advance_velocity(velocity, buoyancy)
        set_coefficients(strip_coef, velocity, buoyancy, gate)
        for t in range(tracers):
            strip_mix[t] = transport(strip_v[t], strip_coef, LANES)
        for group in range(levels // 8):
            level = slice(group * 8, group * 8 + 8)
            strip_v[:, level, :] = react(
                strip_mix[:, level, :], strip_coef[6, level], light[level], matrix, tracers
            )
    for index, field in enumerate((velocity, buoyancy)):
        low = jnp.logical_and(result, even_lane)
        high = jnp.logical_and(result, odd == 1)
        ub_out[index, :, :LANES] = jnp.where(low, field, ub_out[index, :, :LANES])
        ub_out[index, :, own - LANES :] = jnp.where(high, field, ub_out[index, :, own - LANES :])
    fresh = jnp.logical_and(result, edge_wet)
    for t in range(tracers):
        kept = out_v[t, :, slot_edge].astype(jnp.float32)
        out_v[t, :, slot_edge] = jnp.where(fresh, strip_v[t], kept).astype(jnp.bfloat16)


def finish(t_v, ub_v, t_out, u_out, b_out, sems):
    copies = [
        pltpu.make_async_copy(t_v, t_out, sems.at[0]),
        pltpu.make_async_copy(ub_v.at[0], u_out, sems.at[1]),
        pltpu.make_async_copy(ub_v.at[1], b_out, sems.at[2]),
    ]
    for copy in copies:
        copy.start()
    for copy in copies:
        copy.wait()


def on_device(ocean_u, ocean_b, tracers, wet_tiles, kinetic_matrix):
    levels, own = ocean_u.shape
    count, _, slots = tracers.shape
    padded = count + count % 2
    wide = slots + LANES
    domain = own + 2 * LANES
    f32, bf16 = jnp.float32, jnp.bfloat16
    hbm = pl.BlockSpec(memory_space=pltpu.HBM)
    vmem = pl.BlockSpec(memory_space=pltpu.VMEM)
    operands = [
        pltpu.with_memory_space_constraint(x, pltpu.HBM)
        for x in (ocean_u, ocean_b, tracers, wet_tiles, kinetic_matrix)
    ]
    main, ub = pl.pallas_call(
        functools.partial(kernel, lax.axis_size("sec"), lax.axis_size("tile")),
        out_shape=(
            jax.ShapeDtypeStruct(tracers.shape, bf16),
            jax.ShapeDtypeStruct((2, levels, own), f32),
        ),
        in_specs=[hbm] * 5,
        out_specs=(vmem, vmem),
        scratch_shapes=[
            pltpu.VMEM((levels, domain), f32),
            pltpu.VMEM((levels, domain), f32),
            pltpu.VMEM(tracers.shape, bf16),
            pltpu.VMEM(kinetic_matrix.shape, f32),
            pltpu.SMEM(wet_tiles.shape, jnp.int32),
            pltpu.VMEM((count, levels, LANES), bf16),
            pltpu.VMEM((2, levels, LANES), f32),
            pltpu.VMEM((levels, LANES), f32),
            pltpu.VMEM((levels, LANES), f32),
            pltpu.VMEM((levels, LANES), f32),
            pltpu.VMEM((levels, LANES), f32),
            pltpu.VMEM((2, levels, LANES), f32),
            pltpu.VMEM((2, levels, LANES), f32),
            pltpu.VMEM((count, levels, wide), f32),
            pltpu.VMEM((padded, levels, wide), f32),
            pltpu.VMEM((levels, wide), f32),
            pltpu.VMEM((7, levels, wide), f32),
            pltpu.VMEM((count, levels, LANES), f32),
            pltpu.VMEM((padded, levels, LANES), f32),
            pltpu.VMEM((7, levels, LANES), f32),
            pltpu.SemaphoreType.DMA((7,)),
            pltpu.SemaphoreType.DMA,
            pltpu.SemaphoreType.DMA((6,)),
            pltpu.SemaphoreType.DMA((6,)),
            pltpu.SemaphoreType.REGULAR,
        ],
        compiler_params=pltpu.CompilerParams(
            collective_id=0, has_side_effects=True, vmem_limit_bytes=40 * 2**20
        ),
    )(*operands)
    return pl.pallas_call(
        finish,
        out_shape=(
            jax.ShapeDtypeStruct(tracers.shape, bf16),
            jax.ShapeDtypeStruct(ocean_u.shape, f32),
            jax.ShapeDtypeStruct(ocean_b.shape, f32),
        ),
        in_specs=[vmem, vmem],
        out_specs=(hbm, hbm, hbm),
        scratch_shapes=[pltpu.SemaphoreType.DMA((3,))],
        compiler_params=pltpu.CompilerParams(vmem_limit_bytes=2**20),
    )(main, ub)


def solution(mesh):
    flat = ("sec", "tile")
    placed = (P(None, flat), P(None, flat), P(None, None, flat), P(), P())
    return jax.shard_map(
        on_device,
        mesh=mesh,
        in_specs=placed,
        out_specs=(P(None, None, flat), P(None, flat), P(None, flat)),
        check_vma=False,
    )
```

time: 33.9 us -> 23.1 us (0.68)
  local copies, waits for them, and re-layouts: 6.56 us -> 0 us
  Pallas kernels: 26.4 us -> 22.4 us
    unnamed x13 -> x0, local copies, waits for them, and re-layouts: 6.56 us -> none
    pallas_call x1, Pallas kernels: 26.4 us -> 21.3 us  [on_device(): pl.pallas_call(functools.partial(kernel, lax.axis_size('sec'), lax.axis_s...]
    pallas_call x0 -> x1, Pallas kernels: none -> 1 us  [on_device(): pl.pallas_call(finish, out_shape=(jax.ShapeDtypeStruct(tracers.shape, bf1...]
where the time goes in v2:
time: 23.1 us; the launch traced here: 23 us
  Pallas kernels  22.4 us (97%)
  between operations  0.64 us (3%)
    pallas_call x1, Pallas kernels, on_device(): pl.pallas_call(functools.partial(kernel, lax.axis_size('sec'), lax.axis_s...  21.3 us
    pallas_call x1, Pallas kernels, on_device(): pl.pallas_call(finish, out_shape=(jax.ShapeDtypeStruct(tracers.shape, bf1...  1 us

profile of v2, /device:TPU:1, one launch (start us, length us, event | category | flops | bytes accessed | tf_op | source)
XLA Modules:
  0.0 23.0 jit_solution(4526381435528358411)
XLA Ops:
  0.6 21.3 %shard_map.76 = (bf16[17,64,384]{2,1,0:T(8,128)(2,1)S(1)}, f32[2,64,512]{2,1,0:T(8,128)S(1)}) custom-call(f32[64,512]{1,0:T(8,128)} %u_in.1, f32[64,512]{1,0:T(8,128)} %b_in.1, bf16[17,64,384]{2,1,0:T(8,128)(2,1)} %t_in.1, s32[1536]{0:T(1024)} %wet_in.1, f32[17,17]{1,0:T(8,128)} %k_in.1), custom_call_target="tpu_custom_call" | custom-call | tf_op jit(solution)/shard_map/pallas_call | solution.py:393
  22.0 1.0 %shard_map.77 = (bf16[17,64,384]{2,1,0:T(8,128)(2,1)}, f32[64,512]{1,0:T(8,128)}, f32[64,512]{1,0:T(8,128)}) custom-call(bf16[17,64,384]{2,1,0:T(8,128)(2,1)S(1)} %get-tuple-element.5.t_v, f32[2,64,512]{2,1,0:T(8,128)S(1)} %get-tuple-element.6.ub_v), custom_call_target="tpu_custom_call" | custom-call | tf_op jit(solution)/shard_map/pallas_call | solution.py:432

commit v3 on v2

--- a/solution.py
+++ b/solution.py
@@ -112,10 +112,10 @@
 
 def kernel(
     secs, tiles, u_in, b_in, t_in, wet_in, k_in,
-    out_v, ub_out,
+    out_v, ub_out, pack_out, far_out, mask_out, matrix_out,
     u_v, b_v, t_v, k_v, wet_s, edge_t, edge_ub, to_near, to_far, from_near, from_far, tile_in, tile_back,
-    s_v, mix_v, abs_v, coef, strip_v, strip_mix, strip_coef,
-    load_sem, wet_sem, send_sem, recv_sem, ready_sem,
+    s_v, mix_v, abs_v, coef,
+    load_sem, wet_sem, send_sem, recv_sem, far_ready, near_ready,
 ):
     levels = u_in.shape[0]
     tracers = t_in.shape[0]
@@ -133,13 +133,6 @@
     far_flat = lax.rem(device + 2 * odd - 1 + secs * tiles, secs * tiles)
     far = (far_flat // tiles, lax.rem(far_flat, tiles))
 
-    barrier = pltpu.get_barrier_semaphore()
-    pl.semaphore_signal(barrier, inc=1, device_id=partner, device_id_type=MESH)
-
-    @pl.when(odd == 0)
-    def _():
-        pl.semaphore_signal(barrier, inc=1, device_id=far, device_id_type=MESH)
-
     slot_edge = pl.ds(pl.multiple_of((slots - LANES) * odd, LANES), LANES)
     far_edge = pl.ds(pl.multiple_of((own - LANES) * odd, LANES), LANES)
     near_edge = pl.ds(pl.multiple_of((own - LANES) * (1 - odd), LANES), LANES)
@@ -153,7 +146,13 @@
         pltpu.make_async_copy(k_in, k_v, load_sem.at[6]),
         pltpu.make_async_copy(wet_in, wet_s, wet_sem),
     ]
-    for load in loads:
+    for load in loads[:3]:
+        load.start()
+
+    barrier = pltpu.get_barrier_semaphore()
+    greeted = (jnp.where(even_lane, far[0], partner[0]), jnp.where(even_lane, far[1], partner[1]))
+    pl.semaphore_signal(barrier, inc=1, device_id=greeted, device_id_type=MESH)
+    for load in loads[3:]:
         load.start()
 
     def remote(src, dst, index, target):
@@ -166,23 +165,38 @@
     base = 2 * tracers
     for load in loads[:3]:
         load.wait()
-    message = jnp.zeros((levels, LANES), jnp.float32)
-    for t in range(tracers):
-        here = (lane >= 2 * t) & (lane < 2 * t + 2)
-        message = jnp.where(here, pltpu.roll(edge_t[t].astype(jnp.float32), 2 * t + 2 * odd, 1), message)
-    for field in range(2):
-        offset = base + HALO * field
-        here = (lane >= offset) & (lane < offset + HALO)
-        message = jnp.where(here, pltpu.roll(edge_ub[field], offset + HALO * odd, 1), message)
-    to_far[...] = message
-
-    pl.semaphore_wait(barrier, 1 + odd)
+    thin = iota((8, LANES), 1)
+    groups = levels // 8
+    for part in range(3):
+        members = range(8 * part, min(8 * part + 8, tracers))
+        value = None
+        for g in range(groups):
+            level = slice(8 * g, 8 * g + 8)
+            chunk = None
+            for t in members:
+                shift = (16 * g + 2 * (t - 8 * part) + 2 * odd) & (LANES - 1)
+                moved = pltpu.roll(edge_t[t, level, :].astype(jnp.float32), shift, 1)
+                chunk = moved if chunk is None else jnp.where((thin & 15) >= 2 * (t - 8 * part), moved, chunk)
+            if part == 2:
+                for field in range(2):
+                    offset = 2 + HALO * field
+                    moved = pltpu.roll(edge_ub[field, level, :], (16 * g + offset + HALO * odd) & (LANES - 1), 1)
+                    chunk = jnp.where((thin & 15) >= offset, moved, chunk)
+            value = chunk if value is None else jnp.where((thin >> 4) == g, chunk, value)
+        to_far[8 * part : 8 * part + 8, :] = value
+
+    pl.semaphore_wait(barrier, 1)
     send_far = remote(to_far, from_far, 0, far)
 
     @pl.when(odd == 1)
     def _():
-        pl.semaphore_signal(ready_sem, inc=1, device_id=far, device_id_type=MESH)
+        pl.semaphore_signal(far_ready, inc=1, device_id=far, device_id_type=MESH)
         send_far.start()
+        pl.semaphore_wait(near_ready, 1)
+
+    @pl.when(odd == 0)
+    def _():
+        pl.semaphore_signal(near_ready, inc=1, device_id=partner, device_id_type=MESH)
 
     tile_u = remote(u_in.at[:, near_edge], tile_in.at[0], 2, partner)
     tile_b = remote(b_in.at[:, near_edge], tile_in.at[1], 3, partner)
@@ -217,7 +231,16 @@
     coarse = matrix.astype(jnp.bfloat16).astype(jnp.float32)
     matrix = jnp.where(iota((rows, wide), 1) < 2 * rows, coarse, matrix - coarse).astype(jnp.bfloat16)
     mix_v[tracers, :, :] = jnp.zeros(mix_v.shape[1:], jnp.float32)
-    strip_mix[tracers, :, :] = jnp.zeros(strip_mix.shape[1:], jnp.float32)
+    matrix_out[...] = matrix
+
+    for f in range(tracers + 2):
+        value = None
+        for g in range(groups):
+            level = slice(8 * g, 8 * g + 8)
+            part = edge_t[f, level, :].astype(jnp.float32) if f < tracers else edge_ub[f - tracers, level, :]
+            moved = roll(part, 16 * g + 8, 1)
+            value = moved if value is None else jnp.where((thin >> 4) == g, moved, value)
+        pack_out[f] = value
 
     for t in range(tracers):
         s_v[t, :, :slots] = t_v[t].astype(jnp.float32)
@@ -311,7 +334,7 @@
 
     @pl.when(odd == 0)
     def _():
-        pl.semaphore_wait(ready_sem, 1)
+        pl.semaphore_wait(far_ready, 1)
         send_far.start()
 
     for copy in final:
@@ -326,53 +349,137 @@
 
     edge_wet = jnp.where(even_lane, relative[1] == 0, relative[WET_DEV] == OCEAN_DEV - 1)
     halo_wet = jnp.where(even_lane, relative[0] == -1, relative[WET_DEV + 1] == OCEAN_DEV)
-    own_side = jnp.where(even_lane, lane, LANES - 1 - lane) < LANES // 2
-    lit = jnp.where(own_side, edge_wet.astype(jnp.int32), halo_wet.astype(jnp.int32)) == 1
-    ends = jnp.logical_and(edge_wet, halo_wet).astype(jnp.float32)
-    gate = jnp.where(lane == LANES - 1, ends, 1.0)
-    halo_two = jnp.where(even_lane, LANES - 1 - lane, lane) < 2
-    halo_three = jnp.where(even_lane, LANES - 1 - lane, lane) < HALO
-    result = jnp.where(even_lane, lane, LANES - 1 - lane) < 4
+    column = thin & 15
+    distance = jnp.where(even_lane, column - 8, 7 - column)
+    edge_wet, halo_wet = edge_wet.astype(jnp.float32), halo_wet.astype(jnp.float32)
+    mask_out[0] = jnp.where(distance >= 0, edge_wet, halo_wet)
+    mask_out[1] = jnp.where(column == 7, edge_wet * halo_wet, 1.0)
+    mask_out[2] = jnp.zeros((8, LANES), jnp.float32) + edge_wet
     send_far.wait()
-    for t in range(tracers):
-        came = pltpu.roll(from_far[...], 2 * LANES - 2 - 2 * t + 2 * odd, 1)
-        strip_v[t] = jnp.where(halo_two, came, edge_t[t].astype(jnp.float32))
-    strip = []
-    for field in range(2):
-        came = pltpu.roll(from_far[...], 2 * LANES - HALO - base - HALO * field + HALO * odd, 1)
-        strip.append(jnp.where(halo_three, came, edge_ub[field]))
-    velocity, buoyancy = strip
-    for step in range(STEPS):
-        light = absorbed_light(strip_v[0], tri)
-        buoyancy = buoyancy + HEATING * jnp.where(lit, light, 0.0)
-        velocity = advance_velocity(velocity, buoyancy)
-        set_coefficients(strip_coef, velocity, buoyancy, gate)
-        for t in range(tracers):
-            strip_mix[t] = transport(strip_v[t], strip_coef, LANES)
-        for group in range(levels // 8):
-            level = slice(group * 8, group * 8 + 8)
-            strip_v[:, level, :] = react(
-                strip_mix[:, level, :], strip_coef[6, level], light[level], matrix, tracers
-            )
-    for index, field in enumerate((velocity, buoyancy)):
-        low = jnp.logical_and(result, even_lane)
-        high = jnp.logical_and(result, odd == 1)
-        ub_out[index, :, :LANES] = jnp.where(low, field, ub_out[index, :, :LANES])
-        ub_out[index, :, own - LANES :] = jnp.where(high, field, ub_out[index, :, own - LANES :])
-    fresh = jnp.logical_and(result, edge_wet)
-    for t in range(tracers):
-        kept = out_v[t, :, slot_edge].astype(jnp.float32)
-        out_v[t, :, slot_edge] = jnp.where(fresh, strip_v[t], kept).astype(jnp.bfloat16)
-
-
-def finish(t_v, ub_v, t_out, u_out, b_out, sems):
-    copies = [
-        pltpu.make_async_copy(t_v, t_out, sems.at[0]),
-        pltpu.make_async_copy(ub_v.at[0], u_out, sems.at[1]),
-        pltpu.make_async_copy(ub_v.at[1], b_out, sems.at[2]),
-    ]
+    far_out[...] = from_far[...]
+
+
+def finish(
+    t_v, ub_v, pack_v, far_v, mask_v, matrix_v, t_out, u_out, b_out, mix_v, sems,
+):
+    tracers, levels, slots = t_out.shape
+    own = u_out.shape[1]
+    odd = lax.rem(lax.axis_index("tile"), 2)
+    even_lane = odd == 0
+    slot_rest = pl.ds(pl.multiple_of(LANES * (1 - odd), LANES), slots - LANES)
+    own_rest = pl.ds(pl.multiple_of(LANES * (1 - odd), LANES), own - LANES)
+    slot_edge = pl.ds(pl.multiple_of((slots - LANES) * odd, LANES), LANES)
+    far_edge = pl.ds(pl.multiple_of((own - LANES) * odd, LANES), LANES)
+    outs = (u_out, b_out)
+    copies = [pltpu.make_async_copy(t_v.at[:, :, slot_rest], t_out.at[:, :, slot_rest], sems.at[0])]
+    for f in range(2):
+        copies.append(
+            pltpu.make_async_copy(ub_v.at[f, :, own_rest], outs[f].at[:, own_rest], sems.at[1 + f])
+        )
     for copy in copies:
         copy.start()
+
+    shape = (8, LANES)
+    lane = iota(shape, 1)
+    row = iota(shape, 0)
+    column = lane & 15
+    level = 8 * (lane >> 4) + row
+    inside = jnp.where(even_lane, 7 - column, column - 8)
+    halo_two = (inside >= 0) & (inside < 2)
+    halo_three = (inside >= 0) & (inside < HALO)
+
+    def above(x):
+        turned = roll(x, 1, 0)
+        return jnp.where(row == 0, roll(turned, 16, 1), turned)
+
+    def below(x):
+        turned = roll(x, -1, 0)
+        return jnp.where(row == 7, roll(turned, -16, 1), turned)
+
+    def total_from_top(x):
+        for shift in (1, 2, 4):
+            x = x + jnp.where(row >= shift, roll(x, shift, 0), 0.0)
+        groups = jnp.where(lane >= 16, roll(jnp.broadcast_to(x[7:8], shape), 16, 1), 0.0)
+        for shift in (16, 32, 64):
+            groups = groups + jnp.where(lane >= shift, roll(groups, shift, 1), 0.0)
+        return x + groups
+
+    state = []
+    for t in range(tracers):
+        part = far_v[8 * (t // 8) : 8 * (t // 8) + 8, :]
+        came = pltpu.roll(part, (6 - 2 * (t % 8) + 2 * odd) & (LANES - 1), 1)
+        state.append(jnp.where(halo_two, came, pack_v[t]))
+    fields = []
+    for f in range(2):
+        came = pltpu.roll(far_v[16:24, :], 3 - HALO * f + HALO * odd, 1)
+        fields.append(jnp.where(halo_three, came, pack_v[tracers + f]))
+    velocity, buoyancy = fields
+    lit, gate = mask_v[0], DT_TRACER * mask_v[1]
+    mix_v[8 * tracers :, :] = jnp.zeros((8, LANES), jnp.float32)
+    matrix = matrix_v[...]
+    for step in range(STEPS):
+        attenuation = WATER_ATT + PIGMENT_ATT * state[0] * state[0]
+        depth = total_from_top(attenuation)
+        light = SURFACE_LIGHT * (jnp.exp(attenuation - depth) - jnp.exp(-depth))
+        buoyancy = buoyancy + HEATING * lit * light
+        horiz = roll(velocity, 1, 1) + roll(velocity, -1, 1) - 2.0 * velocity
+        upper = jnp.where(level == 0, velocity, above(velocity))
+        lower = jnp.where(level == levels - 1, velocity, below(velocity))
+        press = roll(buoyancy, -1, 1) - buoyancy
+        velocity = velocity + DT_OCEAN * (
+            HORIZ_VISC * horiz + VERT_VISC * (upper + lower - 2.0 * velocity) - PRESSURE * press
+        )
+        shear = velocity - below(velocity)
+        steep = 4.0 * (shear * shear - (buoyancy - below(buoyancy)))
+        spreading = KAPPA_BASE + KAPPA_SPAN / (1.0 + jnp.exp(-steep))
+        spreading = jnp.where(level == levels - 1, 0.0, spreading)
+        spreading_up = jnp.where(level == 0, 0.0, above(spreading))
+        forward = jnp.maximum(velocity, 0.0) * gate
+        backward = jnp.minimum(velocity, 0.0) * gate
+        stay = 1.0 - forward + roll(backward, 1, 1)
+        from_left = roll(forward, 1, 1)
+        keep = 1.0 - DT_MIX * (spreading + spreading_up)
+        warm = KINETIC_DELTA * jnp.exp(THERMAL_GAIN * buoyancy)
+        mixed = []
+        for t in range(tracers):
+            moved = stay * state[t] - backward * roll(state[t], -1, 1) + from_left * roll(state[t], 1, 1)
+            mixed.append(
+                keep * moved + DT_MIX * (spreading * below(moved) + spreading_up * above(moved))
+            )
+            mix_v[8 * t : 8 * t + 8, :] = mixed[t]
+        flat = mix_v[...]
+        high = flat.astype(jnp.bfloat16)
+        low = (flat - high.astype(jnp.float32)).astype(jnp.bfloat16)
+        drift = jnp.dot(
+            matrix, jnp.concatenate([high, low, high], axis=0), preferred_element_type=jnp.float32
+        )
+        state = [mixed[t] + warm * drift[8 * t : 8 * t + 8] for t in range(tracers)]
+        state[0] = state[0] + GROWTH * light
+
+    near_edge = jnp.where(even_lane, lane, LANES - 1 - lane) < 4
+    near_wet = near_edge & (mask_v[2] > 0.5)
+    for f, field in enumerate((velocity, buoyancy)):
+        for g in range(levels // 8):
+            rows = slice(8 * g, 8 * g + 8)
+            kept = ub_v[f, rows, far_edge]
+            ub_v[f, rows, far_edge] = jnp.where(near_edge, roll(field, -16 * g - 8, 1), kept)
+        copies.append(
+            pltpu.make_async_copy(ub_v.at[f, :, far_edge], outs[f].at[:, far_edge], sems.at[3 + f])
+        )
+        copies[-1].start()
+    near_wet = jnp.concatenate([near_wet.astype(jnp.float32)] * 2, axis=0) > 0.5
+    for t in range(tracers):
+        for g in range(levels // 16):
+            rows = slice(16 * g, 16 * g + 16)
+            fresh = jnp.concatenate(
+                [roll(state[t], -32 * g - 8, 1), roll(state[t], -32 * g - 24, 1)], axis=0
+            )
+            kept = t_v[t, rows, slot_edge].astype(jnp.float32)
+            t_v[t, rows, slot_edge] = jnp.where(near_wet, fresh, kept).astype(jnp.bfloat16)
+    copies.append(
+        pltpu.make_async_copy(t_v.at[:, :, slot_edge], t_out.at[:, :, slot_edge], sems.at[5])
+    )
+    copies[-1].start()
     for copy in copies:
         copy.wait()
 
@@ -390,14 +497,19 @@
         pltpu.with_memory_space_constraint(x, pltpu.HBM)
         for x in (ocean_u, ocean_b, tracers, wet_tiles, kinetic_matrix)
     ]
-    main, ub = pl.pallas_call(
+    rows = 8 * padded
+    parts = pl.pallas_call(
         functools.partial(kernel, lax.axis_size("sec"), lax.axis_size("tile")),
         out_shape=(
             jax.ShapeDtypeStruct(tracers.shape, bf16),
             jax.ShapeDtypeStruct((2, levels, own), f32),
+            jax.ShapeDtypeStruct((count + 2, 8, LANES), f32),
+            jax.ShapeDtypeStruct((24, LANES), f32),
+            jax.ShapeDtypeStruct((3, 8, LANES), f32),
+            jax.ShapeDtypeStruct((rows, 3 * rows), bf16),
         ),
         in_specs=[hbm] * 5,
-        out_specs=(vmem, vmem),
+        out_specs=(vmem,) * 6,
         scratch_shapes=[
             pltpu.VMEM((levels, domain), f32),
             pltpu.VMEM((levels, domain), f32),
@@ -407,22 +519,20 @@
             pltpu.VMEM((count, levels, LANES), bf16),
             pltpu.VMEM((2, levels, LANES), f32),
             pltpu.VMEM((levels, LANES), f32),
+            pltpu.VMEM((24, LANES), f32),
             pltpu.VMEM((levels, LANES), f32),
-            pltpu.VMEM((levels, LANES), f32),
-            pltpu.VMEM((levels, LANES), f32),
+            pltpu.VMEM((24, LANES), f32),
             pltpu.VMEM((2, levels, LANES), f32),
             pltpu.VMEM((2, levels, LANES), f32),
             pltpu.VMEM((count, levels, wide), f32),
             pltpu.VMEM((padded, levels, wide), f32),
             pltpu.VMEM((levels, wide), f32),
             pltpu.VMEM((7, levels, wide), f32),
-            pltpu.VMEM((count, levels, LANES), f32),
-            pltpu.VMEM((padded, levels, LANES), f32),
-            pltpu.VMEM((7, levels, LANES), f32),
             pltpu.SemaphoreType.DMA((7,)),
             pltpu.SemaphoreType.DMA,
             pltpu.SemaphoreType.DMA((6,)),
             pltpu.SemaphoreType.DMA((6,)),
+            pltpu.SemaphoreType.REGULAR,
             pltpu.SemaphoreType.REGULAR,
         ],
         compiler_params=pltpu.CompilerParams(
@@ -436,11 +546,11 @@
             jax.ShapeDtypeStruct(ocean_u.shape, f32),
             jax.ShapeDtypeStruct(ocean_b.shape, f32),
         ),
-        in_specs=[vmem, vmem],
+        in_specs=[vmem] * 6,
         out_specs=(hbm, hbm, hbm),
-        scratch_shapes=[pltpu.SemaphoreType.DMA((3,))],
-        compiler_params=pltpu.CompilerParams(vmem_limit_bytes=2**20),
-    )(main, ub)
+        scratch_shapes=[pltpu.VMEM((rows, LANES), f32), pltpu.SemaphoreType.DMA((6,))],
+        compiler_params=pltpu.CompilerParams(vmem_limit_bytes=4 * 2**20),
+    )(*parts)
 
 
 def solution(mesh):

time: 23.1 us -> 22.1 us (0.957)
  Pallas kernels: 22.4 us -> 21.3 us
    pallas_call x1, Pallas kernels: 21.3 us -> 18.9 us  [on_device(): pl.pallas_call(functools.partial(kernel, lax.axis_size('sec'), lax.axis_s...]
    pallas_call x1, Pallas kernels: 1 us -> 2.43 us  [on_device(): pl.pallas_call(finish, out_shape=(jax.ShapeDtypeStruct(tracers.shape, bf1...]
where the time goes in v3:
time: 22.1 us; the launch traced here: 22 us
  Pallas kernels  21.3 us (96%)
  between operations  0.64 us (3%)
    pallas_call x1, Pallas kernels, on_device(): pl.pallas_call(functools.partial(kernel, lax.axis_size('sec'), lax.axis_s...  18.9 us
    pallas_call x1, Pallas kernels, on_device(): pl.pallas_call(finish, out_shape=(jax.ShapeDtypeStruct(tracers.shape, bf1...  2.43 us

profile of v3, /device:TPU:1, one launch (start us, length us, event | category | flops | bytes accessed | tf_op | source)
XLA Modules:
  0.0 22.0 jit_solution(10499042194841102787)
XLA Ops:
  0.6 18.9 %shard_map.76 = (bf16[17,64,384]{2,1,0:T(8,128)(2,1)S(1)}, f32[2,64,512]{2,1,0:T(8,128)S(1)}, f32[19,8,128]{2,1,0:T(8,128)S(1)}, f32[24,128]{1,0:T(8,128)S(1)}, ...) custom-call(f32[64,512]{1,0:T(8,128)} %u_in.1, f32[64,512]{1,0:T(8,128)} %b_in.1, bf16[17,64,384]{2,1,0:T(8,128)(2,1)} %t_in.1, ...), custom_call_target="tpu_custom_call" | custom-call | tf_op jit(solution)/shard_map/pallas_call | solution.py:501
  19.6 2.4 %shard_map.77 = (bf16[17,64,384]{2,1,0:T(8,128)(2,1)}, f32[64,512]{1,0:T(8,128)}, f32[64,512]{1,0:T(8,128)}) custom-call(bf16[17,64,384]{2,1,0:T(8,128)(2,1)S(1)} %get-tuple-element.9.t_v, f32[2,64,512]{2,1,0:T(8,128)S(1)} %get-tuple-element.10.ub_v, f32[19,8,128]{2,1,0:T(8,128)S(1)} %get-tuple-element.11.pack_v, f32[24,128]{1,0:T(8,128)S(1)} %get-tuple-element.12.far_v, ...), custom_call_target="tpu_custom_call" | custom-call | tf_op jit(solution)/shard_map/pallas_call | solution.py:542

commit v4 on v3

--- a/solution.py
+++ b/solution.py
@@ -112,9 +112,9 @@
 
 def kernel(
     secs, tiles, u_in, b_in, t_in, wet_in, k_in,
-    out_v, ub_out, pack_out, far_out, mask_out, matrix_out,
+    out_v, ub_out,
     u_v, b_v, t_v, k_v, wet_s, edge_t, edge_ub, to_near, to_far, from_near, from_far, tile_in, tile_back,
-    s_v, mix_v, abs_v, coef,
+    s_v, mix_v, abs_v, coef, pack_v, thin_mix,
     load_sem, wet_sem, send_sem, recv_sem, far_ready, near_ready,
 ):
     levels = u_in.shape[0]
@@ -231,7 +231,7 @@
     coarse = matrix.astype(jnp.bfloat16).astype(jnp.float32)
     matrix = jnp.where(iota((rows, wide), 1) < 2 * rows, coarse, matrix - coarse).astype(jnp.bfloat16)
     mix_v[tracers, :, :] = jnp.zeros(mix_v.shape[1:], jnp.float32)
-    matrix_out[...] = matrix
+    thin_mix[8 * tracers :, :] = jnp.zeros((8, LANES), jnp.float32)
 
     for f in range(tracers + 2):
         value = None
@@ -240,7 +240,7 @@
             part = edge_t[f, level, :].astype(jnp.float32) if f < tracers else edge_ub[f - tracers, level, :]
             moved = roll(part, 16 * g + 8, 1)
             value = moved if value is None else jnp.where((thin >> 4) == g, moved, value)
-        pack_out[f] = value
+        pack_v[f] = value
 
     for t in range(tracers):
         s_v[t, :, :slots] = t_v[t].astype(jnp.float32)
@@ -352,37 +352,9 @@
     column = thin & 15
     distance = jnp.where(even_lane, column - 8, 7 - column)
     edge_wet, halo_wet = edge_wet.astype(jnp.float32), halo_wet.astype(jnp.float32)
-    mask_out[0] = jnp.where(distance >= 0, edge_wet, halo_wet)
-    mask_out[1] = jnp.where(column == 7, edge_wet * halo_wet, 1.0)
-    mask_out[2] = jnp.zeros((8, LANES), jnp.float32) + edge_wet
-    send_far.wait()
-    far_out[...] = from_far[...]
-
-
-def finish(
-    t_v, ub_v, pack_v, far_v, mask_v, matrix_v, t_out, u_out, b_out, mix_v, sems,
-):
-    tracers, levels, slots = t_out.shape
-    own = u_out.shape[1]
-    odd = lax.rem(lax.axis_index("tile"), 2)
-    even_lane = odd == 0
-    slot_rest = pl.ds(pl.multiple_of(LANES * (1 - odd), LANES), slots - LANES)
-    own_rest = pl.ds(pl.multiple_of(LANES * (1 - odd), LANES), own - LANES)
-    slot_edge = pl.ds(pl.multiple_of((slots - LANES) * odd, LANES), LANES)
-    far_edge = pl.ds(pl.multiple_of((own - LANES) * odd, LANES), LANES)
-    outs = (u_out, b_out)
-    copies = [pltpu.make_async_copy(t_v.at[:, :, slot_rest], t_out.at[:, :, slot_rest], sems.at[0])]
-    for f in range(2):
-        copies.append(
-            pltpu.make_async_copy(ub_v.at[f, :, own_rest], outs[f].at[:, own_rest], sems.at[1 + f])
-        )
-    for copy in copies:
-        copy.start()
-
     shape = (8, LANES)
-    lane = iota(shape, 1)
+    lane = thin
     row = iota(shape, 0)
-    column = lane & 15
     level = 8 * (lane >> 4) + row
     inside = jnp.where(even_lane, 7 - column, column - 8)
     halo_two = (inside >= 0) & (inside < 2)
@@ -404,19 +376,22 @@
             groups = groups + jnp.where(lane >= shift, roll(groups, shift, 1), 0.0)
         return x + groups
 
+    lit = jnp.where(distance >= 0, edge_wet, halo_wet)
+    gate = DT_TRACER * jnp.where(column == 7, edge_wet * halo_wet, 1.0)
+    near_side = jnp.where(even_lane, lane, LANES - 1 - lane) < 4
+    near_wet = jnp.concatenate([jnp.where(near_side, edge_wet, 0.0)] * 2, axis=0) > 0.5
+
+    send_far.wait()
     state = []
     for t in range(tracers):
-        part = far_v[8 * (t // 8) : 8 * (t // 8) + 8, :]
+        part = from_far[8 * (t // 8) : 8 * (t // 8) + 8, :]
         came = pltpu.roll(part, (6 - 2 * (t % 8) + 2 * odd) & (LANES - 1), 1)
         state.append(jnp.where(halo_two, came, pack_v[t]))
     fields = []
     for f in range(2):
-        came = pltpu.roll(far_v[16:24, :], 3 - HALO * f + HALO * odd, 1)
+        came = pltpu.roll(from_far[16:24, :], 3 - HALO * f + HALO * odd, 1)
         fields.append(jnp.where(halo_three, came, pack_v[tracers + f]))
     velocity, buoyancy = fields
-    lit, gate = mask_v[0], DT_TRACER * mask_v[1]
-    mix_v[8 * tracers :, :] = jnp.zeros((8, LANES), jnp.float32)
-    matrix = matrix_v[...]
     for step in range(STEPS):
         attenuation = WATER_ATT + PIGMENT_ATT * state[0] * state[0]
         depth = total_from_top(attenuation)
@@ -446,8 +421,8 @@
             mixed.append(
                 keep * moved + DT_MIX * (spreading * below(moved) + spreading_up * above(moved))
             )
-            mix_v[8 * t : 8 * t + 8, :] = mixed[t]
-        flat = mix_v[...]
+            thin_mix[8 * t : 8 * t + 8, :] = mixed[t]
+        flat = thin_mix[...]
         high = flat.astype(jnp.bfloat16)
         low = (flat - high.astype(jnp.float32)).astype(jnp.bfloat16)
         drift = jnp.dot(
@@ -456,30 +431,29 @@
         state = [mixed[t] + warm * drift[8 * t : 8 * t + 8] for t in range(tracers)]
         state[0] = state[0] + GROWTH * light
 
-    near_edge = jnp.where(even_lane, lane, LANES - 1 - lane) < 4
-    near_wet = near_edge & (mask_v[2] > 0.5)
     for f, field in enumerate((velocity, buoyancy)):
-        for g in range(levels // 8):
+        for g in range(groups):
             rows = slice(8 * g, 8 * g + 8)
-            kept = ub_v[f, rows, far_edge]
-            ub_v[f, rows, far_edge] = jnp.where(near_edge, roll(field, -16 * g - 8, 1), kept)
-        copies.append(
-            pltpu.make_async_copy(ub_v.at[f, :, far_edge], outs[f].at[:, far_edge], sems.at[3 + f])
-        )
-        copies[-1].start()
-    near_wet = jnp.concatenate([near_wet.astype(jnp.float32)] * 2, axis=0) > 0.5
+            kept = ub_out[f, rows, far_edge]
+            ub_out[f, rows, far_edge] = jnp.where(near_side, roll(field, -16 * g - 8, 1), kept)
     for t in range(tracers):
         for g in range(levels // 16):
             rows = slice(16 * g, 16 * g + 16)
             fresh = jnp.concatenate(
                 [roll(state[t], -32 * g - 8, 1), roll(state[t], -32 * g - 24, 1)], axis=0
             )
-            kept = t_v[t, rows, slot_edge].astype(jnp.float32)
-            t_v[t, rows, slot_edge] = jnp.where(near_wet, fresh, kept).astype(jnp.bfloat16)
-    copies.append(
-        pltpu.make_async_copy(t_v.at[:, :, slot_edge], t_out.at[:, :, slot_edge], sems.at[5])
-    )
-    copies[-1].start()
+            kept = out_v[t, rows, slot_edge].astype(jnp.float32)
+            out_v[t, rows, slot_edge] = jnp.where(near_wet, fresh, kept).astype(jnp.bfloat16)
+
+
+def finish(t_v, ub_v, t_out, u_out, b_out, sems):
+    copies = [
+        pltpu.make_async_copy(t_v, t_out, sems.at[0]),
+        pltpu.make_async_copy(ub_v.at[0], u_out, sems.at[1]),
+        pltpu.make_async_copy(ub_v.at[1], b_out, sems.at[2]),
+    ]
+    for copy in copies:
+        copy.start()
     for copy in copies:
         copy.wait()
 
@@ -503,13 +477,9 @@
         out_shape=(
             jax.ShapeDtypeStruct(tracers.shape, bf16),
             jax.ShapeDtypeStruct((2, levels, own), f32),
-            jax.ShapeDtypeStruct((count + 2, 8, LANES), f32),
-            jax.ShapeDtypeStruct((24, LANES), f32),
-            jax.ShapeDtypeStruct((3, 8, LANES), f32),
-            jax.ShapeDtypeStruct((rows, 3 * rows), bf16),
         ),
         in_specs=[hbm] * 5,
-        out_specs=(vmem,) * 6,
+        out_specs=(vmem,) * 2,
         scratch_shapes=[
             pltpu.VMEM((levels, domain), f32),
             pltpu.VMEM((levels, domain), f32),
@@ -528,6 +498,8 @@
             pltpu.VMEM((padded, levels, wide), f32),
             pltpu.VMEM((levels, wide), f32),
             pltpu.VMEM((7, levels, wide), f32),
+            pltpu.VMEM((count + 2, 8, LANES), f32),
+            pltpu.VMEM((rows, LANES), f32),
             pltpu.SemaphoreType.DMA((7,)),
             pltpu.SemaphoreType.DMA,
             pltpu.SemaphoreType.DMA((6,)),
@@ -546,10 +518,10 @@
             jax.ShapeDtypeStruct(ocean_u.shape, f32),
             jax.ShapeDtypeStruct(ocean_b.shape, f32),
         ),
-        in_specs=[vmem] * 6,
+        in_specs=[vmem] * 2,
         out_specs=(hbm, hbm, hbm),
-        scratch_shapes=[pltpu.VMEM((rows, LANES), f32), pltpu.SemaphoreType.DMA((6,))],
-        compiler_params=pltpu.CompilerParams(vmem_limit_bytes=4 * 2**20),
+        scratch_shapes=[pltpu.SemaphoreType.DMA((3,))],
+        compiler_params=pltpu.CompilerParams(vmem_limit_bytes=2**20),
     )(*parts)
 
 

time: 22.1 us -> 22.3 us (level)
  Pallas kernels: 21.3 us -> 21.6 us
    pallas_call x1, Pallas kernels: 18.9 us -> 20.6 us  [on_device(): pl.pallas_call(functools.partial(kernel, lax.axis_size('sec'), lax.axis_s...]
    pallas_call x1, Pallas kernels: 2.43 us -> 1 us  [on_device(): pl.pallas_call(finish, out_shape=(jax.ShapeDtypeStruct(tracers.shape, bf1...]
where the time goes in v4:
time: 22.3 us; the launch traced here: 22.2 us
  Pallas kernels  21.6 us (97%)
  between operations  0.64 us (3%)
    pallas_call x1, Pallas kernels, on_device(): pl.pallas_call(functools.partial(kernel, lax.axis_size('sec'), lax.axis_s...  20.6 us
    pallas_call x1, Pallas kernels, on_device(): pl.pallas_call(finish, out_shape=(jax.ShapeDtypeStruct(tracers.shape, bf1...  1 us

profile of v4, /device:TPU:1, one launch (start us, length us, event | category | flops | bytes accessed | tf_op | source)
XLA Modules:
  0.0 22.2 jit_solution(13626931696996936162)
XLA Ops:
  0.6 20.6 %shard_map.76 = (bf16[17,64,384]{2,1,0:T(8,128)(2,1)S(1)}, f32[2,64,512]{2,1,0:T(8,128)S(1)}) custom-call(f32[64,512]{1,0:T(8,128)} %u_in.1, f32[64,512]{1,0:T(8,128)} %b_in.1, bf16[17,64,384]{2,1,0:T(8,128)(2,1)} %t_in.1, s32[1536]{0:T(1024)} %wet_in.1, f32[17,17]{1,0:T(8,128)} %k_in.1), custom_call_target="tpu_custom_call" | custom-call | tf_op jit(solution)/shard_map/pallas_call | solution.py:475
  21.2 1.0 %shard_map.77 = (bf16[17,64,384]{2,1,0:T(8,128)(2,1)}, f32[64,512]{1,0:T(8,128)}, f32[64,512]{1,0:T(8,128)}) custom-call(bf16[17,64,384]{2,1,0:T(8,128)(2,1)S(1)} %get-tuple-element.5.t_v, f32[2,64,512]{2,1,0:T(8,128)S(1)} %get-tuple-element.6.ub_v), custom_call_target="tpu_custom_call" | custom-call | tf_op jit(solution)/shard_map/pallas_call | solution.py:514

commit v5 on v4

--- a/solution.py
+++ b/solution.py
@@ -69,12 +69,16 @@
     return velocity + DT_OCEAN * (HORIZ_VISC * horiz + VERT_VISC * vert - PRESSURE * press)
 
 
+def diffusivity(shear, settled):
+    steep = 4.0 * (shear * shear - settled)
+    return KAPPA_BASE + KAPPA_SPAN / (1.0 + jnp.exp(-steep))
+
+
 def set_coefficients(coef, face_u, warmth, gate):
     level = iota(face_u.shape, 0)
     shear = face_u - roll(face_u, -1, 0)
     stratified = warmth - roll(warmth, -1, 0)
-    steep = 4.0 * (shear * shear - stratified)
-    spreading = KAPPA_BASE + KAPPA_SPAN / (1.0 + jnp.exp(-steep))
+    spreading = diffusivity(shear, stratified)
     spreading = jnp.where(level == face_u.shape[0] - 1, 0.0, spreading)
     spreading_up = jnp.where(level == 0, 0.0, roll(spreading, 1, 0))
     gate = DT_TRACER * gate
@@ -167,22 +171,26 @@
         load.wait()
     thin = iota((8, LANES), 1)
     groups = levels // 8
+    frame = (thin + (LANES - 8 + 2 * odd)) & (LANES - 1)
+    last_frame = (thin + (LANES - 8 + HALO * odd)) & (LANES - 1)
     for part in range(3):
-        members = range(8 * part, min(8 * part + 8, tracers))
+        spots = frame if part < 2 else last_frame
+        within = spots & 15
         value = None
         for g in range(groups):
             level = slice(8 * g, 8 * g + 8)
-            chunk = None
-            for t in members:
-                shift = (16 * g + 2 * (t - 8 * part) + 2 * odd) & (LANES - 1)
-                moved = pltpu.roll(edge_t[t, level, :].astype(jnp.float32), shift, 1)
-                chunk = moved if chunk is None else jnp.where((thin & 15) >= 2 * (t - 8 * part), moved, chunk)
-            if part == 2:
-                for field in range(2):
-                    offset = 2 + HALO * field
-                    moved = pltpu.roll(edge_ub[field, level, :], (16 * g + offset + HALO * odd) & (LANES - 1), 1)
-                    chunk = jnp.where((thin & 15) >= offset, moved, chunk)
-            value = chunk if value is None else jnp.where((thin >> 4) == g, chunk, value)
+            natural = 16 * g + 8
+            if part < 2:
+                chunk = None
+                for k in range(8):
+                    moved = roll(edge_t[8 * part + k, level, :].astype(jnp.float32), natural + 2 * k, 1)
+                    chunk = moved if chunk is None else jnp.where(within >= 2 * k, moved, chunk)
+            else:
+                chunk = roll(edge_ub[0, level, :], natural, 1)
+                chunk = jnp.where(within >= HALO, roll(edge_ub[1, level, :], natural + HALO, 1), chunk)
+                moved = roll(edge_t[tracers - 1, level, :].astype(jnp.float32), natural + 2 * HALO, 1)
+                chunk = jnp.where(within >= 2 * HALO, moved, chunk)
+            value = chunk if value is None else jnp.where((spots >> 4) == g, chunk, value)
         to_far[8 * part : 8 * part + 8, :] = value
 
     pl.semaphore_wait(barrier, 1)
@@ -371,10 +379,11 @@
     def total_from_top(x):
         for shift in (1, 2, 4):
             x = x + jnp.where(row >= shift, roll(x, shift, 0), 0.0)
-        groups = jnp.where(lane >= 16, roll(jnp.broadcast_to(x[7:8], shape), 16, 1), 0.0)
-        for shift in (16, 32, 64):
-            groups = groups + jnp.where(lane >= shift, roll(groups, shift, 1), 0.0)
-        return x + groups
+        whole = jnp.broadcast_to(x[7:8], shape)
+        parts = [jnp.where(lane >= 16 * k, roll(whole, 16 * k, 1), 0.0) for k in range(1, levels // 8)]
+        while len(parts) > 1:
+            parts = [sum(parts[k : k + 2]) for k in range(0, len(parts), 2)]
+        return x + parts[0]
 
     lit = jnp.where(distance >= 0, edge_wet, halo_wet)
     gate = DT_TRACER * jnp.where(column == 7, edge_wet * halo_wet, 1.0)
@@ -385,11 +394,11 @@
     state = []
     for t in range(tracers):
         part = from_far[8 * (t // 8) : 8 * (t // 8) + 8, :]
-        came = pltpu.roll(part, (6 - 2 * (t % 8) + 2 * odd) & (LANES - 1), 1)
+        came = roll(part, -2 * (t % 8) if t < 16 else -2 * HALO, 1)
         state.append(jnp.where(halo_two, came, pack_v[t]))
     fields = []
     for f in range(2):
-        came = pltpu.roll(from_far[16:24, :], 3 - HALO * f + HALO * odd, 1)
+        came = roll(from_far[16:24, :], -HALO * f, 1)
         fields.append(jnp.where(halo_three, came, pack_v[tracers + f]))
     velocity, buoyancy = fields
     for step in range(STEPS):
@@ -404,11 +413,10 @@
         velocity = velocity + DT_OCEAN * (
             HORIZ_VISC * horiz + VERT_VISC * (upper + lower - 2.0 * velocity) - PRESSURE * press
         )
-        shear = velocity - below(velocity)
-        steep = 4.0 * (shear * shear - (buoyancy - below(buoyancy)))
-        spreading = KAPPA_BASE + KAPPA_SPAN / (1.0 + jnp.exp(-steep))
-        spreading = jnp.where(level == levels - 1, 0.0, spreading)
-        spreading_up = jnp.where(level == 0, 0.0, above(spreading))
+        shear, settled = velocity - below(velocity), buoyancy - below(buoyancy)
+        spreading = jnp.where(level == levels - 1, 0.0, diffusivity(shear, settled))
+        shear, settled = above(velocity) - velocity, above(buoyancy) - buoyancy
+        spreading_up = jnp.where(level == 0, 0.0, diffusivity(shear, settled))
         forward = jnp.maximum(velocity, 0.0) * gate
         backward = jnp.minimum(velocity, 0.0) * gate
         stay = 1.0 - forward + roll(backward, 1, 1)

time: 22.3 us -> 21.8 us (0.978)
  Pallas kernels: 21.6 us -> 21.1 us
    pallas_call x1, Pallas kernels: 20.6 us -> 20.1 us  [on_device(): pl.pallas_call(functools.partial(kernel, lax.axis_size('sec'), lax.axis_s...]
where the time goes in v5:
time: 21.8 us; the launch traced here: 21.7 us
  Pallas kernels  21.1 us (97%)
  between operations  0.64 us (3%)
    pallas_call x1, Pallas kernels, on_device(): pl.pallas_call(functools.partial(kernel, lax.axis_size('sec'), lax.axis_s...  20.1 us
    pallas_call x1, Pallas kernels, on_device(): pl.pallas_call(finish, out_shape=(jax.ShapeDtypeStruct(tracers.shape, bf1...  1 us

profile of v5, /device:TPU:1, one launch (start us, length us, event | category | flops | bytes accessed | tf_op | source)
XLA Modules:
  0.0 21.7 jit_solution(1100199898766724488)
XLA Ops:
  0.6 20.1 %shard_map.76 = (bf16[17,64,384]{2,1,0:T(8,128)(2,1)S(1)}, f32[2,64,512]{2,1,0:T(8,128)S(1)}) custom-call(f32[64,512]{1,0:T(8,128)} %u_in.1, f32[64,512]{1,0:T(8,128)} %b_in.1, bf16[17,64,384]{2,1,0:T(8,128)(2,1)} %t_in.1, s32[1536]{0:T(1024)} %wet_in.1, f32[17,17]{1,0:T(8,128)} %k_in.1), custom_call_target="tpu_custom_call" | custom-call | tf_op jit(solution)/shard_map/pallas_call | solution.py:483
  20.7 1.0 %shard_map.77 = (bf16[17,64,384]{2,1,0:T(8,128)(2,1)}, f32[64,512]{1,0:T(8,128)}, f32[64,512]{1,0:T(8,128)}) custom-call(bf16[17,64,384]{2,1,0:T(8,128)(2,1)S(1)} %get-tuple-element.5.t_v, f32[2,64,512]{2,1,0:T(8,128)S(1)} %get-tuple-element.6.ub_v), custom_call_target="tpu_custom_call" | custom-call | tf_op jit(solution)/shard_map/pallas_call | solution.py:522

commit v6 on v5

--- a/solution.py
+++ b/solution.py
@@ -144,10 +144,10 @@
         pltpu.make_async_copy(t_in.at[:, :, slot_edge], edge_t, load_sem.at[0]),
         pltpu.make_async_copy(u_in.at[:, far_edge], edge_ub.at[0], load_sem.at[1]),
         pltpu.make_async_copy(b_in.at[:, far_edge], edge_ub.at[1], load_sem.at[2]),
-        pltpu.make_async_copy(t_in, t_v, load_sem.at[3]),
-        pltpu.make_async_copy(u_in, u_v.at[:, pl.ds(0, own)], load_sem.at[4]),
-        pltpu.make_async_copy(b_in, b_v.at[:, pl.ds(0, own)], load_sem.at[5]),
-        pltpu.make_async_copy(k_in, k_v, load_sem.at[6]),
+        pltpu.make_async_copy(t_in, t_v, load_sem.at[0]),
+        pltpu.make_async_copy(u_in, u_v.at[:, pl.ds(0, own)], load_sem.at[1]),
+        pltpu.make_async_copy(b_in, b_v.at[:, pl.ds(0, own)], load_sem.at[2]),
+        pltpu.make_async_copy(k_in, k_v, load_sem.at[3]),
         pltpu.make_async_copy(wet_in, wet_s, wet_sem),
     ]
     for load in loads[:3]:
@@ -156,8 +156,6 @@
     barrier = pltpu.get_barrier_semaphore()
     greeted = (jnp.where(even_lane, far[0], partner[0]), jnp.where(even_lane, far[1], partner[1]))
     pl.semaphore_signal(barrier, inc=1, device_id=greeted, device_id_type=MESH)
-    for load in loads[3:]:
-        load.start()
 
     def remote(src, dst, index, target):
         return pltpu.make_async_remote_copy(
@@ -169,6 +167,8 @@
     base = 2 * tracers
     for load in loads[:3]:
         load.wait()
+    for load in loads[3:]:
+        load.start()
     thin = iota((8, LANES), 1)
     groups = levels // 8
     frame = (thin + (LANES - 8 + 2 * odd)) & (LANES - 1)
@@ -508,7 +508,7 @@
             pltpu.VMEM((7, levels, wide), f32),
             pltpu.VMEM((count + 2, 8, LANES), f32),
             pltpu.VMEM((rows, LANES), f32),
-            pltpu.SemaphoreType.DMA((7,)),
+            pltpu.SemaphoreType.DMA((4,)),
             pltpu.SemaphoreType.DMA,
             pltpu.SemaphoreType.DMA((6,)),
             pltpu.SemaphoreType.DMA((6,)),

time: 21.8 us -> 21.8 us (level)
  no operation moved by 1% of the time
where the time goes in v6:
time: 21.8 us; the launch traced here: 21.7 us
  Pallas kernels  21 us (96%)
  between operations  0.64 us (3%)
    pallas_call x1, Pallas kernels, on_device(): pl.pallas_call(functools.partial(kernel, lax.axis_size('sec'), lax.axis_s...  20 us
    pallas_call x1, Pallas kernels, on_device(): pl.pallas_call(finish, out_shape=(jax.ShapeDtypeStruct(tracers.shape, bf1...  1 us

profile of v6, /device:TPU:1, one launch (start us, length us, event | category | flops | bytes accessed | tf_op | source)
XLA Modules:
  0.0 21.7 jit_solution(10361933143655180326)
XLA Ops:
  0.6 20.0 %shard_map.76 = (bf16[17,64,384]{2,1,0:T(8,128)(2,1)S(1)}, f32[2,64,512]{2,1,0:T(8,128)S(1)}) custom-call(f32[64,512]{1,0:T(8,128)} %u_in.1, f32[64,512]{1,0:T(8,128)} %b_in.1, bf16[17,64,384]{2,1,0:T(8,128)(2,1)} %t_in.1, s32[1536]{0:T(1024)} %wet_in.1, f32[17,17]{1,0:T(8,128)} %k_in.1), custom_call_target="tpu_custom_call" | custom-call | tf_op jit(solution)/shard_map/pallas_call | solution.py:483
  20.7 1.0 %shard_map.77 = (bf16[17,64,384]{2,1,0:T(8,128)(2,1)}, f32[64,512]{1,0:T(8,128)}, f32[64,512]{1,0:T(8,128)}) custom-call(bf16[17,64,384]{2,1,0:T(8,128)(2,1)S(1)} %get-tuple-element.5.t_v, f32[2,64,512]{2,1,0:T(8,128)S(1)} %get-tuple-element.6.ub_v), custom_call_target="tpu_custom_call" | custom-call | tf_op jit(solution)/shard_map/pallas_call | solution.py:522

commit v7 on v5

--- a/solution.py
+++ b/solution.py
@@ -164,6 +164,16 @@
             src_ref=src, dst_ref=dst, send_sem=send_sem.at[index], recv_sem=recv_sem.at[index],
             device_id=target, device_id_type=MESH,
         )
+
+    pl.semaphore_wait(barrier, 1)
+
+    @pl.when(odd == 1)
+    def _():
+        pl.semaphore_signal(far_ready, inc=1, device_id=far, device_id_type=MESH)
+
+    @pl.when(odd == 0)
+    def _():
+        pl.semaphore_signal(near_ready, inc=1, device_id=partner, device_id_type=MESH)
 
     lane = iota((levels, LANES), 1)
     base = 2 * tracers
@@ -193,18 +203,12 @@
             value = chunk if value is None else jnp.where((spots >> 4) == g, chunk, value)
         to_far[8 * part : 8 * part + 8, :] = value
 
-    pl.semaphore_wait(barrier, 1)
     send_far = remote(to_far, from_far, 0, far)
 
     @pl.when(odd == 1)
     def _():
-        pl.semaphore_signal(far_ready, inc=1, device_id=far, device_id_type=MESH)
         send_far.start()
         pl.semaphore_wait(near_ready, 1)
-
-    @pl.when(odd == 0)
-    def _():
-        pl.semaphore_signal(near_ready, inc=1, device_id=partner, device_id_type=MESH)
 
     tile_u = remote(u_in.at[:, near_edge], tile_in.at[0], 2, partner)
     tile_b = remote(b_in.at[:, near_edge], tile_in.at[1], 3, partner)
@@ -268,15 +272,15 @@
     tri = (iota((levels, levels), 0) >= iota((levels, levels), 1)).astype(jnp.float32)
     abs_v[:, :slots] = absorbed_light(s_v[0, :, :slots], tri)
 
-    send_near.wait()
+    send_near.wait_recv()
     halo_two = jnp.where(even_lane, lane, LANES - 1 - lane) < 2
     halo_three = jnp.where(even_lane, lane, LANES - 1 - lane) < HALO
     for t in range(tracers):
         came = pltpu.roll(from_near[...], 2 * LANES - 2 * t - 2 * odd, 1)
         s_v[t, :, slots:] = jnp.where(halo_two, came, 0.0)
     abs_v[:, slots:] = absorbed_light(s_v[0, :, slots:], tri)
-    tile_u.wait()
-    tile_b.wait()
+    tile_u.wait_recv()
+    tile_b.wait_recv()
     for field, offset, whole in ((u_v, base, tile_in[0]), (b_v, base + HALO, tile_in[1])):
         came = pltpu.roll(from_near[...], 2 * LANES - offset - HALO * odd, 1)
         near = jnp.where(halo_three, came, 0.0)
@@ -346,7 +350,7 @@
         send_far.start()
 
     for copy in final:
-        copy.wait()
+        copy.wait_recv()
     for field, index in ((u_v, 0), (b_v, 1)):
         back = tile_back[index]
         low_given = jnp.logical_and(odd == 1, spot_left == 0)
@@ -390,7 +394,7 @@
     near_side = jnp.where(even_lane, lane, LANES - 1 - lane) < 4
     near_wet = jnp.concatenate([jnp.where(near_side, edge_wet, 0.0)] * 2, axis=0) > 0.5
 
-    send_far.wait()
+    send_far.wait_recv()
     state = []
     for t in range(tracers):
         part = from_far[8 * (t // 8) : 8 * (t // 8) + 8, :]
@@ -452,6 +456,8 @@
             )
             kept = out_v[t, rows, slot_edge].astype(jnp.float32)
             out_v[t, rows, slot_edge] = jnp.where(near_wet, fresh, kept).astype(jnp.bfloat16)
+    for copy in (send_near, tile_u, tile_b, *final, send_far):
+        copy.wait_send()
 
 
 def finish(t_v, ub_v, t_out, u_out, b_out, sems):

time: 21.8 us -> 21.9 us (level)
  no operation moved by 1% of the time
where the time goes in v7:
time: 21.9 us; the launch traced here: 21.7 us
  Pallas kernels  21.1 us (96%)
  between operations  0.64 us (3%)
    pallas_call x1, Pallas kernels, on_device(): pl.pallas_call(functools.partial(kernel, lax.axis_size('sec'), lax.axis_s...  20.1 us
    pallas_call x1, Pallas kernels, on_device(): pl.pallas_call(finish, out_shape=(jax.ShapeDtypeStruct(tracers.shape, bf1...  1 us

profile of v7, /device:TPU:1, one launch (start us, length us, event | category | flops | bytes accessed | tf_op | source)
XLA Modules:
  0.0 21.7 jit_solution(348146700797428823)
XLA Ops:
  0.6 20.1 %shard_map.76 = (bf16[17,64,384]{2,1,0:T(8,128)(2,1)S(1)}, f32[2,64,512]{2,1,0:T(8,128)S(1)}) custom-call(f32[64,512]{1,0:T(8,128)} %u_in.1, f32[64,512]{1,0:T(8,128)} %b_in.1, bf16[17,64,384]{2,1,0:T(8,128)(2,1)} %t_in.1, s32[1536]{0:T(1024)} %wet_in.1, f32[17,17]{1,0:T(8,128)} %k_in.1), custom_call_target="tpu_custom_call" | custom-call | tf_op jit(solution)/shard_map/pallas_call | solution.py:489
  20.7 1.0 %shard_map.77 = (bf16[17,64,384]{2,1,0:T(8,128)(2,1)}, f32[64,512]{1,0:T(8,128)}, f32[64,512]{1,0:T(8,128)}) custom-call(bf16[17,64,384]{2,1,0:T(8,128)(2,1)S(1)} %get-tuple-element.5.t_v, f32[2,64,512]{2,1,0:T(8,128)S(1)} %get-tuple-element.6.ub_v), custom_call_target="tpu_custom_call" | custom-call | tf_op jit(solution)/shard_map/pallas_call | solution.py:528

commit v8 on v7

--- a/solution.py
+++ b/solution.py
@@ -118,7 +118,7 @@
     secs, tiles, u_in, b_in, t_in, wet_in, k_in,
     out_v, ub_out,
     u_v, b_v, t_v, k_v, wet_s, edge_t, edge_ub, to_near, to_far, from_near, from_far, tile_in, tile_back,
-    s_v, mix_v, abs_v, coef, pack_v, thin_mix,
+    s_v, mix_v, abs_v, coef, pack_v, splat_v,
     load_sem, wet_sem, send_sem, recv_sem, far_ready, near_ready,
 ):
     levels = u_in.shape[0]
@@ -141,22 +141,24 @@
     far_edge = pl.ds(pl.multiple_of((own - LANES) * odd, LANES), LANES)
     near_edge = pl.ds(pl.multiple_of((own - LANES) * (1 - odd), LANES), LANES)
     loads = [
-        pltpu.make_async_copy(t_in.at[:, :, slot_edge], edge_t, load_sem.at[0]),
-        pltpu.make_async_copy(u_in.at[:, far_edge], edge_ub.at[0], load_sem.at[1]),
-        pltpu.make_async_copy(b_in.at[:, far_edge], edge_ub.at[1], load_sem.at[2]),
+        pltpu.make_async_copy(u_in.at[:, far_edge], edge_ub.at[0], load_sem.at[0]),
+        pltpu.make_async_copy(b_in.at[:, far_edge], edge_ub.at[1], load_sem.at[1]),
+        pltpu.make_async_copy(t_in.at[16:, :, slot_edge], edge_t.at[16:], load_sem.at[2]),
+        pltpu.make_async_copy(t_in.at[:8, :, slot_edge], edge_t.at[:8], load_sem.at[7]),
+        pltpu.make_async_copy(t_in.at[8:16, :, slot_edge], edge_t.at[8:16], load_sem.at[8]),
         pltpu.make_async_copy(t_in, t_v, load_sem.at[3]),
         pltpu.make_async_copy(u_in, u_v.at[:, pl.ds(0, own)], load_sem.at[4]),
         pltpu.make_async_copy(b_in, b_v.at[:, pl.ds(0, own)], load_sem.at[5]),
         pltpu.make_async_copy(k_in, k_v, load_sem.at[6]),
         pltpu.make_async_copy(wet_in, wet_s, wet_sem),
     ]
-    for load in loads[:3]:
+    for load in loads[:5]:
         load.start()
 
     barrier = pltpu.get_barrier_semaphore()
     greeted = (jnp.where(even_lane, far[0], partner[0]), jnp.where(even_lane, far[1], partner[1]))
     pl.semaphore_signal(barrier, inc=1, device_id=greeted, device_id_type=MESH)
-    for load in loads[3:]:
+    for load in loads[5:]:
         load.start()
 
     def remote(src, dst, index, target):
@@ -177,13 +179,13 @@
 
     lane = iota((levels, LANES), 1)
     base = 2 * tracers
-    for load in loads[:3]:
-        load.wait()
     thin = iota((8, LANES), 1)
     groups = levels // 8
     frame = (thin + (LANES - 8 + 2 * odd)) & (LANES - 1)
     last_frame = (thin + (LANES - 8 + HALO * odd)) & (LANES - 1)
-    for part in range(3):
+    for part in (2, 0, 1):
+        for load in loads[3 + part : 4 + part] if part < 2 else loads[:3]:
+            load.wait()
         spots = frame if part < 2 else last_frame
         within = spots & 15
         value = None
@@ -215,7 +217,7 @@
     tile_u.start()
     tile_b.start()
 
-    for load in loads[3:6]:
+    for load in loads[5:8]:
         load.wait()
     message = jnp.zeros((levels, LANES), jnp.float32)
     for t in range(tracers):
@@ -230,7 +232,7 @@
     send_near = remote(to_near, from_near, 1, partner)
     send_near.start()
 
-    loads[6].wait()
+    loads[8].wait()
     rows = 8 * padded
     wide = 3 * rows
     spread = ((iota((rows, tracers), 0) >> 3) == iota((rows, tracers), 1)).astype(jnp.float32)
@@ -243,7 +245,9 @@
     coarse = matrix.astype(jnp.bfloat16).astype(jnp.float32)
     matrix = jnp.where(iota((rows, wide), 1) < 2 * rows, coarse, matrix - coarse).astype(jnp.bfloat16)
     mix_v[tracers, :, :] = jnp.zeros(mix_v.shape[1:], jnp.float32)
-    thin_mix[8 * tracers :, :] = jnp.zeros((8, LANES), jnp.float32)
+    for i in range(tracers):
+        for k in range(tracers):
+            splat_v[tracers * i + k] = jnp.broadcast_to(k_v[i : i + 1, k : k + 1], (8, LANES))
 
     for f in range(tracers + 2):
         value = None
@@ -257,7 +261,7 @@
     for t in range(tracers):
         s_v[t, :, :slots] = t_v[t].astype(jnp.float32)
 
-    loads[7].wait()
+    loads[9].wait()
     listed = [
         wet_s[lax.rem(device * WET_DEV + total_wet + j, total_wet)] for j in range(-1, WET_DEV + 1)
     ]
@@ -433,14 +437,12 @@
             mixed.append(
                 keep * moved + DT_MIX * (spreading * below(moved) + spreading_up * above(moved))
             )
-            thin_mix[8 * t : 8 * t + 8, :] = mixed[t]
-        flat = thin_mix[...]
-        high = flat.astype(jnp.bfloat16)
-        low = (flat - high.astype(jnp.float32)).astype(jnp.bfloat16)
-        drift = jnp.dot(
-            matrix, jnp.concatenate([high, low, high], axis=0), preferred_element_type=jnp.float32
-        )
-        state = [mixed[t] + warm * drift[8 * t : 8 * t + 8] for t in range(tracers)]
+        state = []
+        for t in range(tracers):
+            sums = [splat_v[tracers * t + k] * mixed[k] for k in range(2)]
+            for k in range(2, tracers):
+                sums[k % 2] = sums[k % 2] + splat_v[tracers * t + k] * mixed[k]
+            state.append(mixed[t] + warm * (sums[0] + sums[1]))
         state[0] = state[0] + GROWTH * light
 
     for f, field in enumerate((velocity, buoyancy)):
@@ -485,7 +487,6 @@
         pltpu.with_memory_space_constraint(x, pltpu.HBM)
         for x in (ocean_u, ocean_b, tracers, wet_tiles, kinetic_matrix)
     ]
-    rows = 8 * padded
     parts = pl.pallas_call(
         functools.partial(kernel, lax.axis_size("sec"), lax.axis_size("tile")),
         out_shape=(
@@ -513,8 +514,8 @@
             pltpu.VMEM((levels, wide), f32),
             pltpu.VMEM((7, levels, wide), f32),
             pltpu.VMEM((count + 2, 8, LANES), f32),
-            pltpu.VMEM((rows, LANES), f32),
-            pltpu.SemaphoreType.DMA((7,)),
+            pltpu.VMEM((count * count, 8, LANES), f32),
+            pltpu.SemaphoreType.DMA((9,)),
             pltpu.SemaphoreType.DMA,
             pltpu.SemaphoreType.DMA((6,)),
             pltpu.SemaphoreType.DMA((6,)),

time: 21.9 us -> 21.7 us (level)
  no operation moved by 1% of the time
where the time goes in v8:
time: 21.7 us; the launch traced here: 21.6 us
  Pallas kernels  20.9 us (96%)
  between operations  0.64 us (3%)
    pallas_call x1, Pallas kernels, on_device(): pl.pallas_call(functools.partial(kernel, lax.axis_size('sec'), lax.axis_s...  19.9 us
    pallas_call x1, Pallas kernels, on_device(): pl.pallas_call(finish, out_shape=(jax.ShapeDtypeStruct(tracers.shape, bf1...  1 us

profile of v8, /device:TPU:1, one launch (start us, length us, event | category | flops | bytes accessed | tf_op | source)
XLA Modules:
  0.0 21.6 jit_solution(6447022570706797029)
XLA Ops:
  0.6 19.9 %shard_map.76 = (bf16[17,64,384]{2,1,0:T(8,128)(2,1)S(1)}, f32[2,64,512]{2,1,0:T(8,128)S(1)}) custom-call(f32[64,512]{1,0:T(8,128)} %u_in.1, f32[64,512]{1,0:T(8,128)} %b_in.1, bf16[17,64,384]{2,1,0:T(8,128)(2,1)} %t_in.1, s32[1536]{0:T(1024)} %wet_in.1, f32[17,17]{1,0:T(8,128)} %k_in.1), custom_call_target="tpu_custom_call" | custom-call | tf_op jit(solution)/shard_map/pallas_call | solution.py:490
  20.6 1.0 %shard_map.77 = (bf16[17,64,384]{2,1,0:T(8,128)(2,1)}, f32[64,512]{1,0:T(8,128)}, f32[64,512]{1,0:T(8,128)}) custom-call(bf16[17,64,384]{2,1,0:T(8,128)(2,1)S(1)} %get-tuple-element.5.t_v, f32[2,64,512]{2,1,0:T(8,128)S(1)} %get-tuple-element.6.ub_v), custom_call_target="tpu_custom_call" | custom-call | tf_op jit(solution)/shard_map/pallas_call | solution.py:529

commit v9 on v8

--- a/solution.py
+++ b/solution.py
@@ -183,6 +183,9 @@
     groups = levels // 8
     frame = (thin + (LANES - 8 + 2 * odd)) & (LANES - 1)
     last_frame = (thin + (LANES - 8 + HALO * odd)) & (LANES - 1)
+    send_far = [
+        remote(to_far.at[pl.ds(8 * p, 8), :], from_far.at[pl.ds(8 * p, 8), :], (0, 6, 7)[p], far) for p in range(3)
+    ]
     for part in (2, 0, 1):
         for load in loads[3 + part : 4 + part] if part < 2 else loads[:3]:
             load.wait()
@@ -205,11 +208,12 @@
             value = chunk if value is None else jnp.where((spots >> 4) == g, chunk, value)
         to_far[8 * part : 8 * part + 8, :] = value
 
-    send_far = remote(to_far, from_far, 0, far)
+        @pl.when(odd == 1)
+        def _(copy=send_far[part]):
+            copy.start()
 
     @pl.when(odd == 1)
     def _():
-        send_far.start()
         pl.semaphore_wait(near_ready, 1)
 
     tile_u = remote(u_in.at[:, near_edge], tile_in.at[0], 2, partner)
@@ -351,7 +355,8 @@
     @pl.when(odd == 0)
     def _():
         pl.semaphore_wait(far_ready, 1)
-        send_far.start()
+        for copy in send_far:
+            copy.start()
 
     for copy in final:
         copy.wait_recv()
@@ -398,7 +403,8 @@
     near_side = jnp.where(even_lane, lane, LANES - 1 - lane) < 4
     near_wet = jnp.concatenate([jnp.where(near_side, edge_wet, 0.0)] * 2, axis=0) > 0.5
 
-    send_far.wait_recv()
+    for copy in send_far:
+        copy.wait_recv()
     state = []
     for t in range(tracers):
         part = from_far[8 * (t // 8) : 8 * (t // 8) + 8, :]
@@ -458,7 +464,7 @@
             )
             kept = out_v[t, rows, slot_edge].astype(jnp.float32)
             out_v[t, rows, slot_edge] = jnp.where(near_wet, fresh, kept).astype(jnp.bfloat16)
-    for copy in (send_near, tile_u, tile_b, *final, send_far):
+    for copy in (send_near, tile_u, tile_b, *final, *send_far):
         copy.wait_send()
 
 
@@ -517,8 +523,8 @@
             pltpu.VMEM((count * count, 8, LANES), f32),
             pltpu.SemaphoreType.DMA((9,)),
             pltpu.SemaphoreType.DMA,
-            pltpu.SemaphoreType.DMA((6,)),
-            pltpu.SemaphoreType.DMA((6,)),
+            pltpu.SemaphoreType.DMA((8,)),
+            pltpu.SemaphoreType.DMA((8,)),
             pltpu.SemaphoreType.REGULAR,
             pltpu.SemaphoreType.REGULAR,
         ],

time: 21.7 us -> 21.7 us (level)
  no operation moved by 1% of the time
where the time goes in v9:
time: 21.7 us; the launch traced here: 21.5 us
  Pallas kernels  20.9 us (96%)
  between operations  0.64 us (3%)
    pallas_call x1, Pallas kernels, on_device(): pl.pallas_call(functools.partial(kernel, lax.axis_size('sec'), lax.axis_s...  19.9 us
    pallas_call x1, Pallas kernels, on_device(): pl.pallas_call(finish, out_shape=(jax.ShapeDtypeStruct(tracers.shape, bf1...  1 us

profile of v9, /device:TPU:1, one launch (start us, length us, event | category | flops | bytes accessed | tf_op | source)
XLA Modules:
  0.0 21.5 jit_solution(2356101066117765349)
XLA Ops:
  0.6 19.9 %shard_map.76 = (bf16[17,64,384]{2,1,0:T(8,128)(2,1)S(1)}, f32[2,64,512]{2,1,0:T(8,128)S(1)}) custom-call(f32[64,512]{1,0:T(8,128)} %u_in.1, f32[64,512]{1,0:T(8,128)} %b_in.1, bf16[17,64,384]{2,1,0:T(8,128)(2,1)} %t_in.1, s32[1536]{0:T(1024)} %wet_in.1, f32[17,17]{1,0:T(8,128)} %k_in.1), custom_call_target="tpu_custom_call" | custom-call | tf_op jit(solution)/shard_map/pallas_call | solution.py:496
  20.5 1.0 %shard_map.77 = (bf16[17,64,384]{2,1,0:T(8,128)(2,1)}, f32[64,512]{1,0:T(8,128)}, f32[64,512]{1,0:T(8,128)}) custom-call(bf16[17,64,384]{2,1,0:T(8,128)(2,1)S(1)} %get-tuple-element.5.t_v, f32[2,64,512]{2,1,0:T(8,128)S(1)} %get-tuple-element.6.ub_v), custom_call_target="tpu_custom_call" | custom-call | tf_op jit(solution)/shard_map/pallas_call | solution.py:535

commit v10 on v9

--- a/solution.py
+++ b/solution.py
@@ -403,13 +403,14 @@
     near_side = jnp.where(even_lane, lane, LANES - 1 - lane) < 4
     near_wet = jnp.concatenate([jnp.where(near_side, edge_wet, 0.0)] * 2, axis=0) > 0.5
 
-    for copy in send_far:
-        copy.wait_recv()
-    state = []
-    for t in range(tracers):
+    def arrived(t):
         part = from_far[8 * (t // 8) : 8 * (t // 8) + 8, :]
         came = roll(part, -2 * (t % 8) if t < 16 else -2 * HALO, 1)
-        state.append(jnp.where(halo_two, came, pack_v[t]))
+        return jnp.where(halo_two, came, pack_v[t])
+
+    send_far[2].wait_recv()
+    send_far[0].wait_recv()
+    state = [arrived(t) for t in range(8)]
     fields = []
     for f in range(2):
         came = roll(from_far[16:24, :], -HALO * f, 1)
@@ -437,6 +438,9 @@
         from_left = roll(forward, 1, 1)
         keep = 1.0 - DT_MIX * (spreading + spreading_up)
         warm = KINETIC_DELTA * jnp.exp(THERMAL_GAIN * buoyancy)
+        if step == 0:
+            send_far[1].wait_recv()
+            state += [arrived(t) for t in range(8, tracers)]
         mixed = []
         for t in range(tracers):
             moved = stay * state[t] - backward * roll(state[t], -1, 1) + from_left * roll(state[t], 1, 1)

time: 21.7 us -> 21.7 us (level)
  no operation moved by 1% of the time
where the time goes in v10:
time: 21.7 us; the launch traced here: 21.5 us
  Pallas kernels  20.9 us (96%)
  between operations  0.64 us (3%)
    pallas_call x1, Pallas kernels, on_device(): pl.pallas_call(functools.partial(kernel, lax.axis_size('sec'), lax.axis_s...  19.9 us
    pallas_call x1, Pallas kernels, on_device(): pl.pallas_call(finish, out_shape=(jax.ShapeDtypeStruct(tracers.shape, bf1...  1 us

profile of v10, /device:TPU:1, one launch (start us, length us, event | category | flops | bytes accessed | tf_op | source)
XLA Modules:
  0.0 21.5 jit_solution(1399506769886940449)
XLA Ops:
  0.6 19.9 %shard_map.76 = (bf16[17,64,384]{2,1,0:T(8,128)(2,1)S(1)}, f32[2,64,512]{2,1,0:T(8,128)S(1)}) custom-call(f32[64,512]{1,0:T(8,128)} %u_in.1, f32[64,512]{1,0:T(8,128)} %b_in.1, bf16[17,64,384]{2,1,0:T(8,128)(2,1)} %t_in.1, s32[1536]{0:T(1024)} %wet_in.1, f32[17,17]{1,0:T(8,128)} %k_in.1), custom_call_target="tpu_custom_call" | custom-call | tf_op jit(solution)/shard_map/pallas_call | solution.py:500
  20.5 1.0 %shard_map.77 = (bf16[17,64,384]{2,1,0:T(8,128)(2,1)}, f32[64,512]{1,0:T(8,128)}, f32[64,512]{1,0:T(8,128)}) custom-call(bf16[17,64,384]{2,1,0:T(8,128)(2,1)S(1)} %get-tuple-element.5.t_v, f32[2,64,512]{2,1,0:T(8,128)S(1)} %get-tuple-element.6.ub_v), custom_call_target="tpu_custom_call" | custom-call | tf_op jit(solution)/shard_map/pallas_call | solution.py:539
